TPU v7x, 256 devices: a whole 4x4x8 slice. The times are simulated.
256 devices in a mesh: gx: 4 (over z_lo, core), gy: 16 (over x, z_hi), gz: 4 (over y).
Axes of the slice: x: 4, y: 4, z: 8 (z_hi: 4, z_lo: 2; z = z_hi * 2 + z_lo), core: 2. Of those that a mesh axis runs over, the one named last changes fastest.
Arguments:
- displacement: float32 [3, 32, 512, 1024], P(None, 'gx', 'gy', 'gz'), may hold values from -1.5 to 1.5
- velocity: float32 [3, 32, 512, 1024], P(None, 'gx', 'gy', 'gz'), may hold values from -6 to 6
- density: float32 [16, 256, 512], P('gx', 'gy', 'gz'), may hold values from 0.5 to 2
- energy: float32 [16, 256, 512], P('gx', 'gy', 'gz'), may hold values from 0.2 to 24
- region: int32 [16, 256, 512], P('gx', 'gy', 'gz'), may hold values from 0 to 3
- heat_ratio: float32 [4], replicated, may hold values from 1.3 to 3
- tracer: float32 [16, 256, 512], P('gx', 'gy', 'gz'), may hold values from -6 to 6
Outputs:
- new_velocity: float32 [3, 32, 512, 1024], P(None, 'gx', 'gy', 'gz')
- relaxed_mesh: float32 [3, 32, 512, 1024], P(None, 'gx', 'gy', 'gz')
- remapped: float32 [16, 256, 512], P('gx', 'gy', 'gz')
All inputs are finite; a program needn't handle non-finite values.
Results may differ from a plain program's by a relative error of at most 0.00002.
Values sent between devices are 32-bit elements; how exact they have to be, the bound alone decides.
No kernel may reach another device: no remote copies, remote signals or barrier semaphores. Data moves between devices by JAX's collectives and lax.ppermute only.
A program may use at most 64 MiB of HBM per device.

v0:
```python
import jax
import jax.numpy as jnp
from jax import lax
from jax.sharding import PartitionSpec as P

courant = 0.5
relax_weight = 0.9
shape_weights = (1.0 / 6.0, 2.0 / 3.0, 1.0 / 6.0)
slope_weights = (-1.0, 0.0, 1.0)


def with_halo(block, sides, width):
    for axis, dim in sides:
        count = lax.axis_size(axis)
        forward = [(i, i + 1) for i in range(count - 1)]
        forward.append((count - 1, 0))
        backward = [(target, source) for source, target in forward]
        low = lax.ppermute(
            lax.slice_in_dim(block, block.shape[dim] - width, None, axis=dim), axis, forward
        )
        high = lax.ppermute(lax.slice_in_dim(block, 0, width, axis=dim), axis, backward)
        block = jnp.concatenate([low, block, high], axis=dim)
    return block


def from_behind(block, axis, distance):
    devices = range(lax.axis_size(axis))
    route = [((i - distance) % len(devices), i) for i in devices]
    return lax.ppermute(block, axis, route)


def weight_column(spatial, column_index):
    listed = [
        slope_weights[column_index] if component == spatial else shape_weights[column_index]
        for component in range(4)
    ]
    return jnp.array(listed, jnp.float32).reshape(4, 1, 1, 1)


def spread_block(extended, position):
    spatial = position - 1
    length = extended.shape[position] - 1
    current = lax.slice_in_dim(extended, 1, length + 1, axis=position)
    earlier = lax.slice_in_dim(extended, 0, length, axis=position)
    first = weight_column(spatial, 0) * current + weight_column(spatial, 2) * earlier
    second = weight_column(spatial, 1) * current
    stacked = jnp.stack([first, second], axis=position + 1)
    target = list(extended.shape)
    target[position] = 2 * length
    return stacked.reshape(target)


def spread_all(extended):
    result = extended
    for position in (1, 2, 3):
        result = spread_block(result, position)
    return result


def sweep_interior(field):
    centre = field[:, 1:-1, 1:-1, 1:-1]
    total = field[:, :-2, 1:-1, 1:-1] + field[:, 2:, 1:-1, 1:-1]
    total = total + field[:, 1:-1, :-2, 1:-1] + field[:, 1:-1, 2:, 1:-1]
    total = total + field[:, 1:-1, 1:-1, :-2] + field[:, 1:-1, 1:-1, 2:]
    return centre + relax_weight * (total / 6.0 - centre)


def relax_once(field):
    widened = with_halo(field, (("gx", 1), ("gy", 2), ("gz", 3)), 1)
    return sweep_interior(widened)


def along(values_wide, position, first_cell, last_cell):
    selector = [slice(1, -1), slice(1, -1), slice(1, -1)]
    selector[position] = slice(first_cell, last_cell)
    return values_wide[tuple(selector)]


def remap_block(tracer, tracer_wide, motion_wide):
    donor_total = jnp.zeros_like(tracer)
    central_total = jnp.zeros_like(tracer)
    floor = tracer
    ceiling = tracer
    for position in range(3):
        behind = along(tracer_wide, position, 0, -1)
        in_front = along(tracer_wide, position, 1, None)
        face_speed = 0.5 * (
            along(motion_wide[position], position, 0, -1)
            + along(motion_wide[position], position, 1, None)
        )
        donor = -(jnp.minimum(face_speed, 0.0) * behind + jnp.maximum(face_speed, 0.0) * in_front)
        central = -face_speed * 0.5 * (behind + in_front)
        length = donor.shape[position]
        donor_total = donor_total + (
            lax.slice_in_dim(donor, 1, length, axis=position)
            - lax.slice_in_dim(donor, 0, length - 1, axis=position)
        )
        central_total = central_total + (
            lax.slice_in_dim(central, 1, length, axis=position)
            - lax.slice_in_dim(central, 0, length - 1, axis=position)
        )
        floor = jnp.minimum(
            jnp.minimum(floor, along(tracer_wide, position, 0, -2)),
            along(tracer_wide, position, 2, None),
        )
        ceiling = jnp.maximum(
            jnp.maximum(ceiling, along(tracer_wide, position, 0, -2)),
            along(tracer_wide, position, 2, None),
        )
    low_order = tracer - donor_total
    high_order = tracer - central_total
    floor = jnp.minimum(floor, low_order)
    ceiling = jnp.maximum(ceiling, low_order)
    return jnp.minimum(jnp.maximum(high_order, floor), ceiling)


def on_device(displacement, velocity, density, energy, region, heat_ratio, tracer):
    labels = jnp.arange(heat_ratio.shape[0], dtype=jnp.int32).reshape(-1, 1, 1, 1)
    member = (region[None] == labels).astype(jnp.float32)
    zone_ratio = jnp.sum(member * heat_ratio.reshape(-1, 1, 1, 1), axis=0)
    pressure = (zone_ratio - 1.0) * density * energy
    sound = jnp.sqrt(zone_ratio * (zone_ratio - 1.0) * energy)
    time_step = courant / lax.pmax(jnp.max(sound), ("gx", "gy", "gz"))
    sources = jnp.stack([pressure, pressure, pressure, density])
    padded = jnp.pad(sources, ((0, 0), (1, 1), (1, 1), (1, 1)))
    partial_value = spread_all(padded)[:, :-1, :-1, :-1]
    rim = from_behind(partial_value[:, -1:], "gx", 1)
    partial_value = jnp.concatenate([partial_value[:, 0:1] + rim, partial_value[:, 1:-1]], axis=1)
    rim = from_behind(partial_value[:, :, -1:], "gy", 1)
    partial_value = jnp.concatenate(
        [partial_value[:, :, 0:1] + rim, partial_value[:, :, 1:-1]], axis=2
    )
    rim = from_behind(partial_value[:, :, :, -1:], "gz", 1)
    assembled = jnp.concatenate(
        [partial_value[:, :, :, 0:1] + rim, partial_value[:, :, :, 1:-1]], axis=3
    )
    new_velocity = velocity + time_step * assembled[:3] / assembled[3:4]
    moved = displacement + time_step * new_velocity
    relaxed_mesh = relax_once(relax_once(moved))
    centres = (relaxed_mesh - moved)[:, 1::2, 1::2, 1::2]
    beside_all = with_halo(
        jnp.concatenate([tracer[None], centres], axis=0), (("gx", 1), ("gy", 2), ("gz", 3)), 1
    )
    tracer_wide = beside_all[0]
    motion_wide = beside_all[1:]
    remapped = remap_block(tracer, tracer_wide, motion_wide)
    return (new_velocity, relaxed_mesh, remapped)


def solution(mesh):
    return jax.shard_map(
        on_device,
        mesh=mesh,
        in_specs=(
            P(None, "gx", "gy", "gz"),
            P(None, "gx", "gy", "gz"),
            P("gx", "gy", "gz"),
            P("gx", "gy", "gz"),
            P("gx", "gy", "gz"),
            P(),
            P("gx", "gy", "gz"),
        ),
        out_specs=(P(None, "gx", "gy", "gz"), P(None, "gx", "gy", "gz"), P("gx", "gy", "gz")),
        check_vma=False,
    )
```

profile of v0, /device:TPU:1, one launch (start us, length us, event | category | flops | bytes accessed | tf_op | source)
XLA Modules:
  0.0 192.8 jit_solution(11905742417377130386)
XLA Ops:
  0.6 0.9 select_reduce_fusion
  1.5 1.4 fusion.42
  2.9 0.9 select_maximum_fusion.1
  3.8 0.8 fusion.34
  4.8 0.3 copy.183
  5.4 0.3 fusion.24
  5.7 0.3 pad_maximum_fusion.2
  6.3 0.4 copy-done.3
  6.7 0.9 fusion.1
  7.6 0.7 pad_maximum_fusion
  8.3 7.3 %copy.185 = f32[4,10,34,129,2]{2,0,4,3,1:T(4,128)} copy(f32[4,10,34,129,2]{3,0,2,1,4:T(4,128)S(1)} %pad_maximum_fusion) | data formatting | bytes 2807040 | tf_op jit(solution)/shard_map/stack | solution.py:47
  15.6 1.3 fusion.54
  16.9 0.3 copy.187
  17.2 3.1 %collective-permute-start = (f32[4,1,33,257]{3,0,2,1:T(4,128)S(1)}, f32[4,1,33,257]{3,0,2,1:T(4,128)S(1)}, u32[]{:S(2)}, u32[]{:S(2)}) collective-permute-start(f32[4,1,33,257]{3,0,2,1:T(4,128)S(1)} %copy.187), channel_id=1, source_target_pairs={{192,0},{0,64},{64,128},{128,192},{193,1},{1,65},{65,129},{129,193... | collective-permute-start | bytes 407096 | tf_op jit(solution)/shard_map/ppermute | solution.py:29
  20.3 4.2 %slice.365 = f32[4,7,33,257]{2,0,3,1:T(4,128)} slice(f32[4,10,34,258]{2,0,3,1:T(4,128)} %bitcast.30), slice={[0:4], [1:8], [0:33], [0:257]} | slice | bytes 1899744 | tf_op jit(solution)/shard_map/slice | solution.py:128
  24.4 0.3 copy.207
  24.7 3.5 %copy.189 = f32[4,7,33,257]{3,1,2,0:T(8,128)S(1)} copy(f32[4,7,33,257]{2,0,3,1:T(4,128)} %slice.365) | data formatting | bytes 1899744 | tf_op jit(solution)/shard_map/slice | solution.py:128
  28.6 3.1 %collective-permute-start.1 = (f32[4,8,1,257]{3,1,2,0:T(8,128)S(1)}, f32[4,8,1,257]{3,1,2,0:T(8,128)S(1)}, u32[]{:S(2)}, u32[]{:S(2)}) collective-permute-start(f32[4,8,1,257]{3,1,2,0:T(8,128)S(1)} %pad_maximum_fusion.44), channel_id=1, source_target_pairs={{60,0},{0,4},{4,8},{8,12},{12,16},{16,20},{20,24},{24,28},{28,32},... | collective-permute-start | bytes 98696 | tf_op jit(solution)/shard_map/ppermute | solution.py:29
  31.6 0.3 pad_maximum_fusion.1
  32.3 5.4 %collective-permute-done.1 = f32[4,8,1,257]{3,1,2,0:T(8,128)S(1)} collective-permute-done((f32[4,8,1,257]{3,1,2,0:T(8,128)S(1)}, f32[4,8,1,257]{3,1,2,0:T(8,128)S(1)}, u32[]{:S(2)}, u32[]{:S(2)}) %collective-permute-start.1) | collective-permute-done | bytes 32928 | tf_op jit(solution)/shard_map/ppermute | solution.py:29
  37.8 1.4 collective-permute-start.2
  39.2 77.8 %pmax.7 = f32[]{:T(128)} all-reduce(f32[]{:T(128)} %get-tuple-element.59), channel_id=1, replica_groups=mesh['gx'=4,'gy'=16,'gz'=4] {'gx','gy','gz'}, use_global_device_ids=true, to_apply=%region_2.0 | all-reduce | flops 1 | bytes 8 | tf_op jit(solution)/shard_map/pmax | solution.py:123
  118.0 0.9 copy-done
  119.1 1.1 multiply_add_fusion
  120.3 2.4 %collective-permute-start.3 = (f32[3,1,32,256]{3,2,1,0:T(8,128)S(1)}, f32[3,1,32,256]{3,2,1,0:T(8,128)S(1)}, u32[]{:S(2)}, u32[]{:S(2)}) collective-permute-start(f32[3,1,32,256]{3,2,1,0:T(8,128)S(1)} %get-tuple-element.36), channel_id=1, source_target_pairs={{0,64},{64,128},{128,192},{192,0},{1,65},{65,129},{129,193},{193,1... | collective-permute-start | bytes 294920 | tf_op jit(solution)/shard_map/ppermute | solution.py:18
  122.6 2.3 %collective-permute-done.3 = f32[3,1,32,256]{3,2,1,0:T(8,128)S(1)} collective-permute-done((f32[3,1,32,256]{3,2,1,0:T(8,128)S(1)}, f32[3,1,32,256]{3,2,1,0:T(8,128)S(1)}, u32[]{:S(2)}, u32[]{:S(2)}) %collective-permute-start.3) | collective-permute-done | bytes 98336 | tf_op jit(solution)/shard_map/ppermute | solution.py:18
  124.9 1.7 collective-permute-done.4
  126.7 0.9 collective-permute-start.5
  127.6 4.9 %collective-permute-start.6 = (f32[3,10,1,256]{3,2,1,0:T(1,128)S(1)}, f32[3,10,1,256]{3,2,1,0:T(1,128)S(1)}, u32[]{:S(2)}, u32[]{:S(2)}) collective-permute-start(f32[3,10,1,256]{3,2,1,0:T(1,128)S(1)} %get-tuple-element.33), channel_id=1, source_target_pairs={{4,0},{8,4},{12,8},{16,12},{20,16},{24,20},{28,24},{32,28},{36,32}... | collective-permute-start | bytes 92168 | tf_op jit(solution)/shard_map/ppermute | solution.py:21
  132.5 1.3 collective-permute-done.5
  134.2 0.3 copy.208
  134.5 0.5 collective-permute-start.7
  135.0 0.3 copy.209
  135.3 2.3 %collective-permute-start.8 = (f32[3,10,34,1]{2,3,1,0:T(1,128)S(1)}, f32[3,10,34,1]{2,3,1,0:T(1,128)S(1)}, u32[]{:S(2)}, u32[]{:S(2)}) collective-permute-start(f32[3,10,34,1]{2,3,1,0:T(1,128)S(1)} %copy.209), channel_id=1, source_target_pairs={{1,0},{2,1},{3,2},{0,3},{5,4},{6,5},{7,6},{4,7},{9,8},{10,9},{11,1... | collective-permute-start | bytes 12248 | tf_op jit(solution)/shard_map/ppermute | solution.py:21
  137.6 0.8 collective-permute-done.7
  138.4 0.3 copy.193
  138.7 0.3 copy.195
  139.0 0.8 fusion.16
  139.8 1.6 collective-permute-start.10
  141.4 1.8 collective-permute-start.9
  143.2 3.2 %collective-permute-done.10 = f32[3,1,32,256]{3,2,1,0:T(8,128)S(1)} collective-permute-done((f32[3,1,32,256]{3,2,1,0:T(8,128)S(1)}, f32[3,1,32,256]{3,2,1,0:T(8,128)S(1)}, u32[]{:S(2)}, u32[]{:S(2)}) %collective-permute-start.10) | collective-permute-done | bytes 98336 | tf_op jit(solution)/shard_map/ppermute | solution.py:21
  146.5 1.3 collective-permute-start.11
  147.8 4.6 %collective-permute-start.12 = (f32[3,10,1,256]{3,2,1,0:T(1,128)S(1)}, f32[3,10,1,256]{3,2,1,0:T(1,128)S(1)}, u32[]{:S(2)}, u32[]{:S(2)}) collective-permute-start(f32[3,10,1,256]{3,2,1,0:T(1,128)S(1)} %get-tuple-element.31), channel_id=1, source_target_pairs={{4,0},{8,4},{12,8},{16,12},{20,16},{24,20},{28,24},{32,28},{36,32}... | collective-permute-start | bytes 92168 | tf_op jit(solution)/shard_map/ppermute | solution.py:21
  152.4 1.5 collective-permute-done.11
  154.3 0.3 copy.210
  154.7 0.3 copy.211
  155.0 3.0 %collective-permute-start.14 = (f32[3,10,34,1]{2,3,1,0:T(1,128)S(1)}, f32[3,10,34,1]{2,3,1,0:T(1,128)S(1)}, u32[]{:S(2)}, u32[]{:S(2)}) collective-permute-start(f32[3,10,34,1]{2,3,1,0:T(1,128)S(1)} %copy.211), channel_id=1, source_target_pairs={{1,0},{2,1},{3,2},{0,3},{5,4},{6,5},{7,6},{4,7},{9,8},{10,9},{11,1... | collective-permute-start | bytes 12248 | tf_op jit(solution)/shard_map/ppermute | solution.py:21
  158.0 0.7 collective-permute-done.13
  158.7 0.3 copy.197
  159.1 0.3 copy.199
  159.4 1.9 %fusion.51 = (f32[3,8,32,256]{3,2,1,0:T(8,128)}, f32[3,8,32,256]{3,2,1,0:T(8,128)}) fusion(f32[3,8,32,256]{3,2,1,0:T(8,128)S(1)} %get-tuple-element.20, f32[3,8,32,256]{3,2,1,0:T(8,128)S(1)} %fusion.16, f32[3,10,34,1]{3,2,1,0:T(8,128)S(1)} %copy.199, f32[3,10,1,256]{3,2,1,0:T(1,128)S(1)} %collective-permute-done.12, ...), kind=kLoop, calls=%fused_computation.155 | loop fusion | flops 5505024 | bytes 3411936 | tf_op jit(solution)/shard_map/sub | solution.py:140
  161.4 7.4 %slice.316 = f32[3,4,16,128]{3,2,1,0:T(8,128)S(1)} slice(f32[3,8,32,256]{3,2,1,0:T(8,128)} %get-tuple-element.18), slice={[0:3:1], [1:8:2], [1:32:2], [1:256:2]} | slice | bytes 196608 | tf_op jit(solution)/shard_map/slice | solution.py:140
  168.8 2.7 %collective-permute-start.15 = (f32[4,1,16,128]{3,2,1,0:T(8,128)S(1)}, f32[4,1,16,128]{3,2,1,0:T(8,128)S(1)}, u32[]{:S(2)}, u32[]{:S(2)}) collective-permute-start(f32[4,1,16,128]{3,2,1,0:T(8,128)S(1)} %get-tuple-element.56), channel_id=1, source_target_pairs={{0,64},{64,128},{128,192},{192,0},{1,65},{65,129},{129,193},{193,1... | collective-permute-start | bytes 98312 | tf_op jit(solution)/shard_map/ppermute | solution.py:18
  171.5 1.0 collective-permute-done.15
  172.6 2.3 %collective-permute-done.16 = f32[4,1,16,128]{3,2,1,0:T(8,128)S(1)} collective-permute-done((f32[4,1,16,128]{3,2,1,0:T(8,128)S(1)}, f32[4,1,16,128]{3,2,1,0:T(8,128)S(1)}, u32[]{:S(2)}, u32[]{:S(2)}) %collective-permute-start.16) | collective-permute-done | bytes 32800 | tf_op jit(solution)/shard_map/ppermute | solution.py:21
  174.9 0.3 collective-permute-start.17
  175.3 5.9 %collective-permute-start.18 = (f32[4,6,1,128]{3,0,2,1:T(4,128)S(1)}, f32[4,6,1,128]{3,0,2,1:T(4,128)S(1)}, u32[]{:S(2)}, u32[]{:S(2)}) collective-permute-start(f32[4,6,1,128]{3,0,2,1:T(4,128)S(1)} %copy.222), channel_id=1, source_target_pairs={{4,0},{8,4},{12,8},{16,12},{20,16},{24,20},{28,24},{32,28},{36,32}... | collective-permute-start | bytes 36872 | tf_op jit(solution)/shard_map/ppermute | solution.py:21
  181.2 1.0 collective-permute-done.17
  182.5 1.2 collective-permute-start.19
  183.8 1.9 collective-permute-start.20
  185.7 5.2 %collective-permute-done.19 = f32[4,6,18,1]{3,0,2,1:T(4,128)S(1)} collective-permute-done((f32[4,6,18,1]{3,0,2,1:T(4,128)S(1)}, f32[4,6,18,1]{3,0,2,1:T(4,128)S(1)}, u32[]{:S(2)}, u32[]{:S(2)}) %collective-permute-start.19) | collective-permute-done | bytes 1760 | tf_op jit(solution)/shard_map/ppermute | solution.py:18
  190.9 0.4 pad_maximum_fusion.42
  191.3 0.3 fusion.59
  192.1 0.8 fusion.49
  (62 shorter events, 3.7 us)
Async XLA Ops:
  4.7 0.7 copy-start.6
  4.7 0.7 copy-start.7
  4.7 0.7 copy-start.8
  6.0 0.7 copy-start.3
  6.0 0.7 copy-start.4
  6.0 0.7 copy-start.5
  17.2 11.1 %collective-permute-start = (f32[4,1,33,257]{3,0,2,1:T(4,128)S(1)}, f32[4,1,33,257]{3,0,2,1:T(4,128)S(1)}, u32[]{:S(2)}, u32[]{:S(2)}) collective-permute-start(f32[4,1,33,257]{3,0,2,1:T(4,128)S(1)} %copy.187), channel_id=1, source_target_pairs={{192,0},{0,64},{64,128},{128,192},{193,1},{1,65},{65,129},{129,193... | collective-permute-start | bytes 407096 | tf_op jit(solution)/shard_map/ppermute | solution.py:29
  28.6 9.1 %collective-permute-start.1 = (f32[4,8,1,257]{3,1,2,0:T(8,128)S(1)}, f32[4,8,1,257]{3,1,2,0:T(8,128)S(1)}, u32[]{:S(2)}, u32[]{:S(2)}) collective-permute-start(f32[4,8,1,257]{3,1,2,0:T(8,128)S(1)} %pad_maximum_fusion.44), channel_id=1, source_target_pairs={{60,0},{0,4},{4,8},{8,12},{12,16},{16,20},{20,24},{24,28},{28,32},... | collective-permute-start | bytes 98696 | tf_op jit(solution)/shard_map/ppermute | solution.py:29
  37.8 79.8 %collective-permute-start.2 = (f32[4,8,32,1]{3,2,1,0:T(8,128)S(1)}, f32[4,8,32,1]{3,2,1,0:T(8,128)S(1)}, u32[]{:S(2)}, u32[]{:S(2)}) collective-permute-start(f32[4,8,32,1]{3,2,1,0:T(8,128)S(1)} %fusion.30), channel_id=1, source_target_pairs={{3,0},{0,1},{1,2},{2,3},{7,4},{4,5},{5,6},{6,7},{11,8},{8,9},{9,10... | collective-permute-start | bytes 12296 | tf_op jit(solution)/shard_map/ppermute | solution.py:29
  117.8 1.1 copy-start
  117.8 1.4 copy-start.1
  120.3 4.7 %collective-permute-start.3 = (f32[3,1,32,256]{3,2,1,0:T(8,128)S(1)}, f32[3,1,32,256]{3,2,1,0:T(8,128)S(1)}, u32[]{:S(2)}, u32[]{:S(2)}) collective-permute-start(f32[3,1,32,256]{3,2,1,0:T(8,128)S(1)} %get-tuple-element.36), channel_id=1, source_target_pairs={{0,64},{64,128},{128,192},{192,0},{1,65},{65,129},{129,193},{193,1... | collective-permute-start | bytes 294920 | tf_op jit(solution)/shard_map/ppermute | solution.py:18
  122.6 4.0 %collective-permute-start.4 = (f32[3,1,32,256]{3,2,1,0:T(8,128)S(1)}, f32[3,1,32,256]{3,2,1,0:T(8,128)S(1)}, u32[]{:S(2)}, u32[]{:S(2)}) collective-permute-start(f32[3,1,32,256]{3,2,1,0:T(8,128)S(1)} %get-tuple-element.37), channel_id=1, source_target_pairs={{64,0},{128,64},{192,128},{0,192},{65,1},{129,65},{193,129},{1,193... | collective-permute-start | bytes 294920 | tf_op jit(solution)/shard_map/ppermute | solution.py:21
  126.7 7.1 %collective-permute-start.5 = (f32[3,10,1,256]{3,2,1,0:T(1,128)S(1)}, f32[3,10,1,256]{3,2,1,0:T(1,128)S(1)}, u32[]{:S(2)}, u32[]{:S(2)}) collective-permute-start(f32[3,10,1,256]{3,2,1,0:T(1,128)S(1)} %get-tuple-element.32), channel_id=1, source_target_pairs={{0,4},{4,8},{8,12},{12,16},{16,20},{20,24},{24,28},{28,32},{32,36}... | collective-permute-start | bytes 92168 | tf_op jit(solution)/shard_map/ppermute | solution.py:18
  127.6 6.2 %collective-permute-start.6 = (f32[3,10,1,256]{3,2,1,0:T(1,128)S(1)}, f32[3,10,1,256]{3,2,1,0:T(1,128)S(1)}, u32[]{:S(2)}, u32[]{:S(2)}) collective-permute-start(f32[3,10,1,256]{3,2,1,0:T(1,128)S(1)} %get-tuple-element.33), channel_id=1, source_target_pairs={{4,0},{8,4},{12,8},{16,12},{20,16},{24,20},{28,24},{32,28},{36,32}... | collective-permute-start | bytes 92168 | tf_op jit(solution)/shard_map/ppermute | solution.py:21
  134.5 3.8 %collective-permute-start.7 = (f32[3,10,34,1]{2,3,1,0:T(1,128)S(1)}, f32[3,10,34,1]{2,3,1,0:T(1,128)S(1)}, u32[]{:S(2)}, u32[]{:S(2)}) collective-permute-start(f32[3,10,34,1]{2,3,1,0:T(1,128)S(1)} %copy.208), channel_id=1, source_target_pairs={{0,1},{1,2},{2,3},{3,0},{4,5},{5,6},{6,7},{7,4},{8,9},{9,10},{10,1... | collective-permute-start | bytes 12248 | tf_op jit(solution)/shard_map/ppermute | solution.py:18
  135.3 3.4 %collective-permute-start.8 = (f32[3,10,34,1]{2,3,1,0:T(1,128)S(1)}, f32[3,10,34,1]{2,3,1,0:T(1,128)S(1)}, u32[]{:S(2)}, u32[]{:S(2)}) collective-permute-start(f32[3,10,34,1]{2,3,1,0:T(1,128)S(1)} %copy.209), channel_id=1, source_target_pairs={{1,0},{2,1},{3,2},{0,3},{5,4},{6,5},{7,6},{4,7},{9,8},{10,9},{11,1... | collective-permute-start | bytes 12248 | tf_op jit(solution)/shard_map/ppermute | solution.py:21
  139.8 6.6 %collective-permute-start.10 = (f32[3,1,32,256]{3,2,1,0:T(8,128)S(1)}, f32[3,1,32,256]{3,2,1,0:T(8,128)S(1)}, u32[]{:S(2)}, u32[]{:S(2)}) collective-permute-start(f32[3,1,32,256]{3,2,1,0:T(8,128)S(1)} %get-tuple-element.35), channel_id=1, source_target_pairs={{64,0},{128,64},{192,128},{0,192},{65,1},{129,65},{193,129},{1,193... | collective-permute-start | bytes 294920 | tf_op jit(solution)/shard_map/ppermute | solution.py:21
  141.4 5.0 %collective-permute-start.9 = (f32[3,1,32,256]{3,2,1,0:T(8,128)S(1)}, f32[3,1,32,256]{3,2,1,0:T(8,128)S(1)}, u32[]{:S(2)}, u32[]{:S(2)}) collective-permute-start(f32[3,1,32,256]{3,2,1,0:T(8,128)S(1)} %get-tuple-element.34), channel_id=1, source_target_pairs={{0,64},{64,128},{128,192},{192,0},{1,65},{65,129},{129,193},{193,1... | collective-permute-start | bytes 294920 | tf_op jit(solution)/shard_map/ppermute | solution.py:18
  146.5 7.4 %collective-permute-start.11 = (f32[3,10,1,256]{3,2,1,0:T(1,128)S(1)}, f32[3,10,1,256]{3,2,1,0:T(1,128)S(1)}, u32[]{:S(2)}, u32[]{:S(2)}) collective-permute-start(f32[3,10,1,256]{3,2,1,0:T(1,128)S(1)} %get-tuple-element.30), channel_id=1, source_target_pairs={{0,4},{4,8},{8,12},{12,16},{16,20},{20,24},{24,28},{28,32},{32,36}... | collective-permute-start | bytes 92168 | tf_op jit(solution)/shard_map/ppermute | solution.py:18
  147.8 6.1 %collective-permute-start.12 = (f32[3,10,1,256]{3,2,1,0:T(1,128)S(1)}, f32[3,10,1,256]{3,2,1,0:T(1,128)S(1)}, u32[]{:S(2)}, u32[]{:S(2)}) collective-permute-start(f32[3,10,1,256]{3,2,1,0:T(1,128)S(1)} %get-tuple-element.31), channel_id=1, source_target_pairs={{4,0},{8,4},{12,8},{16,12},{20,16},{24,20},{28,24},{32,28},{36,32}... | collective-permute-start | bytes 92168 | tf_op jit(solution)/shard_map/ppermute | solution.py:21
  154.6 4.1 %collective-permute-start.13 = (f32[3,10,34,1]{2,3,1,0:T(1,128)S(1)}, f32[3,10,34,1]{2,3,1,0:T(1,128)S(1)}, u32[]{:S(2)}, u32[]{:S(2)}) collective-permute-start(f32[3,10,34,1]{2,3,1,0:T(1,128)S(1)} %copy.210), channel_id=1, source_target_pairs={{0,1},{1,2},{2,3},{3,0},{4,5},{5,6},{6,7},{7,4},{8,9},{9,10},{10,1... | collective-permute-start | bytes 12248 | tf_op jit(solution)/shard_map/ppermute | solution.py:18
  155.0 4.1 %collective-permute-start.14 = (f32[3,10,34,1]{2,3,1,0:T(1,128)S(1)}, f32[3,10,34,1]{2,3,1,0:T(1,128)S(1)}, u32[]{:S(2)}, u32[]{:S(2)}) collective-permute-start(f32[3,10,34,1]{2,3,1,0:T(1,128)S(1)} %copy.211), channel_id=1, source_target_pairs={{1,0},{2,1},{3,2},{0,3},{5,4},{6,5},{7,6},{4,7},{9,8},{10,9},{11,1... | collective-permute-start | bytes 12248 | tf_op jit(solution)/shard_map/ppermute | solution.py:21
  159.4 9.4 %copy-start.2 = (f32[4,16,128]{2,1,0:T(8,128)S(1)}, f32[4,16,128]{2,1,0:T(8,128)}, u32[]{:S(2)}) copy-start(f32[4,16,128]{2,1,0:T(8,128)} %param.22) | copy-start | bytes 98308
  168.8 3.7 %collective-permute-start.15 = (f32[4,1,16,128]{3,2,1,0:T(8,128)S(1)}, f32[4,1,16,128]{3,2,1,0:T(8,128)S(1)}, u32[]{:S(2)}, u32[]{:S(2)}) collective-permute-start(f32[4,1,16,128]{3,2,1,0:T(8,128)S(1)} %get-tuple-element.56), channel_id=1, source_target_pairs={{0,64},{64,128},{128,192},{192,0},{1,65},{65,129},{129,193},{193,1... | collective-permute-start | bytes 98312 | tf_op jit(solution)/shard_map/ppermute | solution.py:18
  171.5 3.3 %collective-permute-start.16 = (f32[4,1,16,128]{3,2,1,0:T(8,128)S(1)}, f32[4,1,16,128]{3,2,1,0:T(8,128)S(1)}, u32[]{:S(2)}, u32[]{:S(2)}) collective-permute-start(f32[4,1,16,128]{3,2,1,0:T(8,128)S(1)} %get-tuple-element.57), channel_id=1, source_target_pairs={{64,0},{128,64},{192,128},{0,192},{65,1},{129,65},{193,129},{1,193... | collective-permute-start | bytes 98312 | tf_op jit(solution)/shard_map/ppermute | solution.py:21
  174.9 7.2 %collective-permute-start.17 = (f32[4,6,1,128]{3,0,2,1:T(4,128)S(1)}, f32[4,6,1,128]{3,0,2,1:T(4,128)S(1)}, u32[]{:S(2)}, u32[]{:S(2)}) collective-permute-start(f32[4,6,1,128]{3,0,2,1:T(4,128)S(1)} %copy.221), channel_id=1, source_target_pairs={{0,4},{4,8},{8,12},{12,16},{16,20},{20,24},{24,28},{28,32},{32,36}... | collective-permute-start | bytes 36872 | tf_op jit(solution)/shard_map/ppermute | solution.py:18
  175.3 7.1 %collective-permute-start.18 = (f32[4,6,1,128]{3,0,2,1:T(4,128)S(1)}, f32[4,6,1,128]{3,0,2,1:T(4,128)S(1)}, u32[]{:S(2)}, u32[]{:S(2)}) collective-permute-start(f32[4,6,1,128]{3,0,2,1:T(4,128)S(1)} %copy.222), channel_id=1, source_target_pairs={{4,0},{8,4},{12,8},{16,12},{20,16},{24,20},{28,24},{32,28},{36,32}... | collective-permute-start | bytes 36872 | tf_op jit(solution)/shard_map/ppermute | solution.py:21
  182.5 8.4 %collective-permute-start.19 = (f32[4,6,18,1]{3,0,2,1:T(4,128)S(1)}, f32[4,6,18,1]{3,0,2,1:T(4,128)S(1)}, u32[]{:S(2)}, u32[]{:S(2)}) collective-permute-start(f32[4,6,18,1]{3,0,2,1:T(4,128)S(1)} %get-tuple-element.52), channel_id=1, source_target_pairs={{0,1},{1,2},{2,3},{3,0},{4,5},{5,6},{6,7},{7,4},{8,9},{9,10},{10,1... | collective-permute-start | bytes 5192 | tf_op jit(solution)/shard_map/ppermute | solution.py:18
  183.8 7.1 %collective-permute-start.20 = (f32[4,6,18,1]{3,0,2,1:T(4,128)S(1)}, f32[4,6,18,1]{3,0,2,1:T(4,128)S(1)}, u32[]{:S(2)}, u32[]{:S(2)}) collective-permute-start(f32[4,6,18,1]{3,0,2,1:T(4,128)S(1)} %get-tuple-element.53), channel_id=1, source_target_pairs={{1,0},{2,1},{3,2},{0,3},{5,4},{6,5},{7,6},{4,7},{9,8},{10,9},{11,1... | collective-permute-start | bytes 5192 | tf_op jit(solution)/shard_map/ppermute | solution.py:21
where the time goes:
time: 194 us; the launch traced here: 193 us
  blocking collectives  77.8 us (40%)
  starting transfers between devices  42.9 us (22%)
  local copies, waits for them, and re-layouts  31 us (16%)
  waiting for transfers between devices  26.5 us (14%)
  other arithmetic  12.9 us (7%)
    pmax x1, blocking collectives, on_device(): time_step = courant / lax.pmax(jnp.max(sound), ('gx', 'gy', 'gz'))  77.8 us
    ppermute x9, starting transfers between devices, with_halo(): lax.ppermute(lax.slice_in_dim(block, 0, width, axis=dim), axis, backward)  24.2 us
    ppermute x9, waiting for transfers between devices, with_halo(): lax.ppermute(lax.slice_in_dim(block, block.shape[dim] - width, None, axis...  13.9 us
    ppermute x9, starting transfers between devices, with_halo(): lax.ppermute(lax.slice_in_dim(block, block.shape[dim] - width, None, axis...  11.1 us
    another operation x3, local copies, waits for them, and re-layouts, spread_block(): stacked = jnp.stack([first, second], axis=position + 1)  7.81 us
    slice x2, local copies, waits for them, and re-layouts, on_device(): partial_value[:, 1:-1]  7.68 us
    ppermute x3, starting transfers between devices, from_behind(): return lax.ppermute(block, axis, route)  7.53 us
    slice x1, local copies, waits for them, and re-layouts, on_device(): centres = (relaxed_mesh - moved)[:, 1::2, 1::2, 1::2]  7.42 us
  transfers between devices with their start and end apart: 21, of which 12 were waited for; matrix products, arithmetic and copies ran while one was open for 5% of the time, Pallas kernels for 0%

commit v1 on v0

v1 whole, which is shorter than its diff:
```python
import jax
import jax.numpy as jnp
from jax import lax
from jax.experimental import pallas as pl
from jax.experimental.pallas import tpu as pltpu
from jax.sharding import PartitionSpec as P

AXES = ("gx", "gy", "gz")
VM = pl.BlockSpec(memory_space=pltpu.VMEM)
SM = pl.BlockSpec(memory_space=pltpu.SMEM)
ANY = pl.BlockSpec(memory_space=pl.ANY)
F32 = jnp.float32

NX, NY, NZ = 8, 32, 256
MX, MY, MZ = 4, 16, 128

X_LOW = [(c, x) for c in range(3) for x in range(-3 if c == 0 else -2, 0)]
X_HIGH = [(c, x) for c in range(3) for x in range(NX, NX + (4 if c == 0 else 2))]
NL, NH = len(X_LOW), len(X_HIGH)
PLANES = [(c, x) for c in range(3) for x in range(-3 if c == 0 else -2, NX + (4 if c == 0 else 2))]
PLANE_AT = {key: i for i, key in enumerate(PLANES)}
NP = len(PLANES)


def low_rows(c, x):
    inside = 0 <= x < NX
    if c == 0:
        return 2 if inside else (1 if x in (-1, NX, NX + 1) else 0)
    if c == 1:
        return 3 if inside else {-1: 1, NX: 2, NX + 1: 1}.get(x, 0)
    return 2 if inside else (1 if x in (-1, NX) else 0)


def high_rows(c, x):
    inside = 0 <= x < NX
    if c == 0:
        return 2 if inside or x in (-1, NX, NX + 1) else (1 if x in (-2, NX + 2) else 0)
    if c == 1:
        return 4 if inside else {-1: 2, NX: 3, NX + 1: 2}.get(x, 0)
    return 2 if inside else (1 if x in (-1, NX) else 0)


def row_table(count):
    table, at = [], 0
    for c, x in PLANES:
        n = count(c, x)
        if n:
            table.append((c, x, at, n))
            at += n
    return table, at


Y_LOW, Y_LOW_N = row_table(low_rows)
Y_HIGH, Y_HIGH_N = row_table(high_rows)
EX = 2 * (MX + 4)
Y_LOW_SIZE = -(-(Y_LOW_N + EX + MX) // 8) * 8
Y_HIGH_SIZE = -(-(Y_HIGH_N + EX + MX) // 8) * 8
ZONE_SLOT = NP
TRACER_SLOT = NP + 2 * (MX + 4)


def step_of(r):
    top = jnp.max(jnp.max(r[...], axis=0, keepdims=True), axis=1, keepdims=True)
    return 0.5 / jnp.sqrt(top)


def first_kernel(ratio, d, v, rho, energy, region, tracer, low, high, most, pressure, zl, zh, sems):
    copies = []

    def copy(src, dst):
        cp = pltpu.make_async_copy(src, dst, sems.at[len(copies)])
        cp.start()
        copies.append(cp)

    at = 0
    for f, array in enumerate((d, v)):
        for c in range(3):
            n = 3 if c == 0 else 2
            off = f * NL + X_LOW.index((c, -n))
            copy(array.at[c, pl.ds(NX - n, n)], low.at[pl.ds(off, n)])
            n = 4 if c == 0 else 2
            off = f * NH + X_HIGH.index((c, NX))
            copy(array.at[c, pl.ds(0, n)], high.at[pl.ds(off, n)])
    top = jnp.zeros((MY, MZ), F32)
    for i in range(MX):
        reg = region[i]
        zone_ratio = jnp.where(
            reg < 2,
            jnp.where(reg == 0, ratio[0], ratio[1]),
            jnp.where(reg == 2, ratio[2], ratio[3]),
        )
        pr = (zone_ratio - 1.0) * rho[i] * energy[i]
        pressure[i] = pr
        top = jnp.maximum(top, zone_ratio * (zone_ratio - 1.0) * energy[i])
        if i < 2:
            zh[0, :MY, i * MZ : (i + 1) * MZ] = pr
            zh[0, MY:, i * MZ : (i + 1) * MZ] = rho[i]
        else:
            zl[0, :MY, (i - 2) * MZ : (i - 1) * MZ] = pr
            zl[0, MY:, (i - 2) * MZ : (i - 1) * MZ] = rho[i]
    zh[1, :MY, :MZ] = tracer[0]
    zl[1, :MY, :MZ] = tracer[MX - 1]
    copy(zl, low.at[pl.ds(2 * NL, 2)])
    copy(zh, high.at[pl.ds(2 * NH, 2)])
    top = jnp.max(jnp.max(top, axis=0, keepdims=True), axis=1, keepdims=True)
    most[...] = jnp.broadcast_to(top, most.shape)
    for cp in copies:
        cp.wait()


def zone_plane(i, own, low, high, which):
    if 0 <= i < MX:
        return own[which][i]
    rows = pl.ds(which * MY, MY)
    if i < 0:
        return low[2 * NL, rows, (i + 2) * MZ : (i + 3) * MZ]
    return high[2 * NH, rows, (i - MX) * MZ : (i - MX + 1) * MZ]


def node_pair(c, x, d, v, low, high):
    if 0 <= x < NX:
        return d.at[c, x], v.at[c, x]
    if x < 0:
        i = X_LOW.index((c, x))
        return low.at[i], low.at[NL + i]
    i = X_HIGH.index((c, x))
    return high.at[i], high.at[NH + i]


def second_kernel(r, d, v, low, high, pressure, rho, tracer, ylow, yhigh):
    step = step_of(r)
    for table, out, start, stop in ((Y_LOW, ylow, None, NY), (Y_HIGH, yhigh, 0, None)):
        for c, x, at, n in table:
            first = NY - n if start is None else 0
            a, b = node_pair(c, x, d, v, low, high)
            out[pl.ds(at, n), :] = a[pl.ds(first, n), :] + step * b[pl.ds(first, n), :]
    for out, base, first, edge in ((ylow, Y_LOW_N, MY - 2, MY - 1), (yhigh, Y_HIGH_N, 0, 0)):
        for i in range(-2, MX + 2):
            for which in range(2):
                lanes = slice(which * MZ, (which + 1) * MZ)
                out[pl.ds(base + 2 * (i + 2), 2), lanes] = zone_plane(
                    i, (pressure, rho), low, high, which
                )[first : first + 2]
        for i in range(MX):
            out[pl.ds(base + EX + i, 1), :MZ] = tracer[i, pl.ds(edge, 1), :]


def third_kernel(
    r, d, v, low, high, pressure, rho, tracer, ylow, yhigh, ext, zones, zlow, zhigh
):
    step = step_of(r)
    lows = {(c, x): (at, n) for c, x, at, n in Y_LOW}
    highs = {(c, x): (at, n) for c, x, at, n in Y_HIGH}
    for e, (c, x) in enumerate(PLANES):
        a, b = node_pair(c, x, d, v, low, high)
        ext[e, pl.ds(8, NY), :] = a[...] + step * b[...]
        if (c, x) in lows:
            at, n = lows[c, x]
            ext[e, pl.ds(8 - n, n), :] = ylow[pl.ds(at, n), :]
        if (c, x) in highs:
            at, n = highs[c, x]
            ext[e, pl.ds(8 + NY, n), :] = yhigh[pl.ds(at, n), :]
    for which in range(2):
        lanes = slice(which * MZ, (which + 1) * MZ)
        for i in range(-2, MX + 2):
            k = which * (MX + 4) + i + 2
            zones[k, pl.ds(4, MY), :] = zone_plane(i, (pressure, rho), low, high, which)
            zones[k, pl.ds(2, 2), :] = ylow[pl.ds(Y_LOW_N + 2 * (i + 2), 2), lanes]
            zones[k, pl.ds(4 + MY, 2), :] = yhigh[pl.ds(Y_HIGH_N + 2 * (i + 2), 2), lanes]
    lane = lax.broadcasted_iota(jnp.int32, (1, 128), 1)
    for tile in range(2):
        zlow[tile] = jnp.zeros((48, 128), F32)
        zhigh[tile] = jnp.zeros((48, 128), F32)
        for s in range(32):
            slot = tile * 32 + s
            if slot >= TRACER_SLOT + MX:
                break
            if slot < ZONE_SLOT:
                left, right, n = ext[slot, :, :128], ext[slot, :, 128:], 48
            elif slot < TRACER_SLOT:
                left = right = zones[slot - ZONE_SLOT]
                n = 24
            else:
                left = right = tracer[slot - TRACER_SLOT]
                n = MY
            here = (lane >= 4 * s) & (lane < 4 * s + 4)
            rows = pl.ds(0, n)
            zhigh[tile, rows] = jnp.where(here, roll(left, 4 * s, 1), zhigh[tile, rows])
            zlow[tile, rows] = jnp.where(here, roll(right, 4 * s + 4, 1), zlow[tile, rows])


def roll(value, by, axis):
    by %= value.shape[axis]
    return pltpu.roll(value, by, axis) if by else value


def pieces(value):
    first = value.astype(jnp.bfloat16)
    rest = value - first.astype(F32)
    second = rest.astype(jnp.bfloat16)
    return first, second, (rest - second.astype(F32)).astype(jnp.bfloat16)


def product(parts, matrix):
    total = None
    for part in parts:
        term = jnp.dot(part, matrix, preferred_element_type=F32)
        total = term if total is None else total + term
    return total


def last_kernel(
    r, v, ext, zones, tracer, low, high, ylow, yhigh, zlow, zhigh,
    velocity, relaxed, remapped,
    moved, once, pz, qx, qy, qz, qm, moves, gathered, result, tz,
):
    step = step_of(r)
    lane = lax.broadcasted_iota(jnp.int32, (1, 128), 1)

    def beside(slot, n, fill):
        tile, s = divmod(slot, 32)
        rows = pl.ds(0, n)
        after = roll(zhigh[tile, rows], -4 * s, 1)
        before = roll(zlow[tile, rows], 124 - 4 * s, 1)
        return jnp.where(lane < 4, after, jnp.where(lane >= 124, before, fill))

    for k in range(2 * (MX + 4)):
        pz[k, :, :MZ] = zones[k]
        pz[k, :, MZ:] = beside(ZONE_SLOT + k, 24, 0.0 if k < MX + 4 else 1.0)
    k = lax.broadcasted_iota(jnp.int32, (2 * MZ, 384), 0)
    n = lax.broadcasted_iota(jnp.int32, (2 * MZ, 384), 1)
    a = jnp.where(n < 320, n, n - 384) - 2 * jnp.where(k < 192, k, k - 256)
    shape = jnp.where((a == 0) | (a == 2), 1.0, jnp.where(a == 1, 4.0, 0.0)).astype(jnp.bfloat16)
    slope = jnp.where(a == 0, -1.0, jnp.where(a == 2, 1.0, 0.0)).astype(jnp.bfloat16)
    half = (MX + 4) * 24
    both = pz[...].reshape(2 * half, 2 * MZ)
    spread = product(pieces(both), shape)
    slanted = product(pieces(both[:half]), slope)
    even, odd = pl.ds(0, 24, stride=2), pl.ds(1, 24, stride=2)

    def interleave(q, i, first, second):
        for t in range(3):
            lanes = slice(128 * t, 128 * t + 128)
            q[3 * i + t, even, :] = first[:, lanes]
            q[3 * i + t, odd, :] = second[:, lanes]

    def whole(q, i):
        return jnp.concatenate([q[3 * i + t] for t in range(3)], axis=1)

    for i in range(MX + 4):
        now = spread[24 * i : 24 * i + 24]
        before = roll(now, 1, 0)
        interleave(qx, i, now + before, 4.0 * now)
        interleave(qy, i, before - now, jnp.zeros((24, 384), F32))
        now = slanted[24 * i : 24 * i + 24]
        interleave(qz, i, now + roll(now, 1, 0), 4.0 * now)
        now = spread[half + 24 * i : half + 24 * i + 24]
        interleave(qm, i, now + roll(now, 1, 0), 4.0 * now)
    for x in range(-3, NX + 4):
        i = x // 2 + 2
        mass = whole(qm, i)
        mass = mass + whole(qm, i - 1) if x % 2 == 0 else 4.0 * mass
        push = 6.0 * step / mass
        for c in range(3):
            if (c, x) not in PLANE_AT:
                continue
            e = PLANE_AT[c, x]
            if c == 0:
                force = whole(qx, i - 1) - whole(qx, i) if x % 2 == 0 else None
            else:
                q = qy if c == 1 else qz
                force = whole(q, i)
                force = force + whole(q, i - 1) if x % 2 == 0 else 4.0 * force
            third = beside(e, 48, 0.0)
            if force is None:
                moved[e, :, :NZ] = ext[e]
                moved[e, :, NZ:] = third
                if 0 <= x < NX:
                    velocity[c, x] = v[c, x]
            else:
                gain = force * push
                moved[e, :, :NZ] = ext[e] + step * gain[:, :NZ]
                moved[e, :, NZ:] = third + step * gain[:, NZ:]
                if 0 <= x < NX:
                    velocity[c, x] = v[c, x] + gain[8 : 8 + NY, :NZ]

    def sweep(ref, e):
        now = ref[e]
        total = ref[e - 1] + ref[e + 1]
        total = total + (roll(now, 1, 0) + roll(now, -1, 0))
        total = total + (roll(now, 1, 1) + roll(now, -1, 1))
        return 0.1 * now + 0.15 * total

    for e, (c, x) in enumerate(PLANES):
        if (c, x - 1) in PLANE_AT and (c, x + 1) in PLANE_AT:
            once[e] = sweep(moved, e)
    at = 0
    for e, (c, x) in enumerate(PLANES):
        inside = 0 <= x < NX
        if not inside and not (c == 0 and x in (-1, NX + 1)):
            continue
        twice = sweep(once, e)
        if inside:
            relaxed[c, x] = twice[8 : 8 + NY, :NZ]
        if x % 2:
            motion = twice - moved[e]
            first, count = (7, 18) if c == 1 else (9, 16)
            for t in range(3):
                lanes = slice(128 * t, 128 * t + 128)
                moves[t] = motion[:, lanes]
                gathered[pl.ds(at, count), lanes] = moves[t, pl.ds(first, count, stride=2), :]
            if c == 1:
                gathered[pl.ds(at + 18, 6), :] = jnp.zeros((6, 384), F32)
            at += 24 if c == 1 else 16
    n = lax.broadcasted_iota(jnp.int32, (384, 2 * MZ), 0)
    k = lax.broadcasted_iota(jnp.int32, (384, 2 * MZ), 1)
    node = jnp.where(n < 320, n, n - 384)
    chosen = (node == 2 * jnp.where(k < 192, k, k - 256) + 1).astype(F32).astype(jnp.bfloat16)
    result[...] = product(pieces(gathered[...]), chosen)

    def flux(speed, behind, here):
        donor = -(jnp.minimum(speed, 0.0) * behind + jnp.maximum(speed, 0.0) * here)
        return donor, -speed * 0.5 * (behind + here)

    y0, z0 = (MX + 2) * 16, (MX + 2) * 16 + MX * 24
    for i in range(MX):
        now = tracer[i]
        tz[pl.ds(8, MY), :] = now
        tz[pl.ds(7, 1), :] = ylow[pl.ds(Y_LOW_N + EX + i, 1), :MZ]
        tz[pl.ds(8 + MY, 1), :] = yhigh[pl.ds(Y_HIGH_N + EX + i, 1), :MZ]
        side = beside(TRACER_SLOT + i, MY, 0.0)
        edge = result[pl.ds(z0 + 16 * i, 16), MZ:]
        middle = result[pl.ds(z0 + 16 * i, 16), :MZ]
        around = (
            (
                tracer[i - 1] if i else low[2 * NL + 1, :MY, :MZ],
                tracer[i + 1] if i < MX - 1 else high[2 * NH + 1, :MY, :MZ],
                result[pl.ds(16 * i, 16), :MZ],
                result[pl.ds(16 * (i + 1), 16), :MZ],
                result[pl.ds(16 * (i + 2), 16), :MZ],
            ),
            (
                tz[pl.ds(7, MY), :],
                tz[pl.ds(9, MY), :],
                result[pl.ds(y0 + 24 * i, 16), :MZ],
                result[pl.ds(y0 + 24 * i + 1, 16), :MZ],
                result[pl.ds(y0 + 24 * i + 2, 16), :MZ],
            ),
            (
                jnp.where(lane == 0, roll(side, 1, 1), roll(now, 1, 1)),
                jnp.where(lane == MZ - 1, roll(side, -1, 1), roll(now, -1, 1)),
                jnp.where(lane == 0, roll(edge, 1, 1), roll(middle, 1, 1)),
                middle,
                jnp.where(lane == MZ - 1, roll(edge, -1, 1), roll(middle, -1, 1)),
            ),
        )
        donors = centrals = None
        floor = ceiling = now
        for behind, front, m0, m1, m2 in around:
            d0, c0 = flux(0.5 * (m0 + m1), behind, now)
            d1, c1 = flux(0.5 * (m1 + m2), now, front)
            donors = d1 - d0 if donors is None else donors + (d1 - d0)
            centrals = c1 - c0 if centrals is None else centrals + (c1 - c0)
            floor = jnp.minimum(jnp.minimum(floor, behind), front)
            ceiling = jnp.maximum(jnp.maximum(ceiling, behind), front)
        low_order = now - donors
        high_order = now - centrals
        floor = jnp.minimum(floor, low_order)
        ceiling = jnp.maximum(ceiling, low_order)
        remapped[i] = jnp.minimum(jnp.maximum(high_order, floor), ceiling)


def shape_of(*dims):
    return jax.ShapeDtypeStruct(dims, F32)


def moved_along(block, axis, by):
    n = lax.axis_size(axis)
    return lax.ppermute(block, axis, [(i, (i + by) % n) for i in range(n)])


def on_device(displacement, velocity, density, energy, region, heat_ratio, tracer):
    n_devices = lax.axis_size(AXES)
    low, high, most, pressure = pl.pallas_call(
        first_kernel,
        name="first",
        in_specs=[SM, ANY, ANY, VM, VM, VM, VM],
        out_specs=[ANY, ANY, VM, VM],
        out_shape=[
            shape_of(2 * NL + 2, NY, NZ),
            shape_of(2 * NH + 2, NY, NZ),
            shape_of(n_devices, 128),
            shape_of(MX, MY, MZ),
        ],
        scratch_shapes=[
            pltpu.VMEM((2, NY, NZ), F32),
            pltpu.VMEM((2, NY, NZ), F32),
            pltpu.SemaphoreType.DMA((14,)),
        ],
    )(heat_ratio, displacement, velocity, density, energy, region, tracer)
    low = moved_along(low, "gx", 1)
    high = moved_along(high, "gx", -1)
    r = lax.all_to_all(most, AXES, 0, 0, tiled=True)
    ylow, yhigh = pl.pallas_call(
        second_kernel,
        name="second",
        in_specs=[VM] * 8,
        out_specs=[VM] * 2,
        out_shape=[shape_of(Y_LOW_SIZE, NZ), shape_of(Y_HIGH_SIZE, NZ)],
    )(r, displacement, velocity, low, high, pressure, density, tracer)
    ylow = moved_along(ylow, "gy", 1)
    yhigh = moved_along(yhigh, "gy", -1)
    ext, zones, zlow, zhigh = pl.pallas_call(
        third_kernel,
        name="third",
        in_specs=[VM] * 10,
        out_specs=[VM] * 4,
        out_shape=[
            shape_of(NP, 48, NZ),
            shape_of(2 * (MX + 4), 24, MZ),
            shape_of(2, 48, 128),
            shape_of(2, 48, 128),
        ],
    )(r, displacement, velocity, low, high, pressure, density, tracer, ylow, yhigh)
    zlow = moved_along(zlow, "gz", 1)
    zhigh = moved_along(zhigh, "gz", -1)
    q = pltpu.VMEM((3 * (MX + 4), 48, 128), F32)
    return pl.pallas_call(
        last_kernel,
        name="last",
        in_specs=[VM] * 11,
        out_specs=[VM] * 3,
        out_shape=[shape_of(3, NX, NY, NZ), shape_of(3, NX, NY, NZ), shape_of(MX, MY, MZ)],
        scratch_shapes=[
            pltpu.VMEM((NP, 48, 384), F32),
            pltpu.VMEM((NP, 48, 384), F32),
            pltpu.VMEM((2 * (MX + 4), 24, 2 * MZ), F32),
            q, q, q, q,
            pltpu.VMEM((3, 48, 128), F32),
            pltpu.VMEM((256, 384), F32),
            pltpu.VMEM((256, 2 * MZ), F32),
            pltpu.VMEM((MY + 16, MZ), F32),
        ],
    )(r, velocity, ext, zones, tracer, low, high, ylow, yhigh, zlow, zhigh)


def solution(mesh):
    node, zone = P(None, "gx", "gy", "gz"), P("gx", "gy", "gz")
    return jax.shard_map(
        on_device,
        mesh=mesh,
        in_specs=(node, node, zone, zone, zone, P(), zone),
        out_specs=(node, node, zone),
        check_vma=False,
    )
```

time: 194 us -> 96.2 us (0.50)
  blocking collectives: 77.8 us -> 26.6 us
  Pallas kernels: 0 us -> 45.8 us
  starting transfers between devices: 42.9 us -> 8.32 us
  local copies, waits for them, and re-layouts: 31 us -> 2.92 us
  waiting for transfers between devices: 26.5 us -> 10.2 us
  other arithmetic: 12.9 us -> 0 us
    pmax x1 -> x0, blocking collectives: 77.8 us -> none  [on_device(): time_step = courant / lax.pmax(jnp.max(sound), ('gx', 'gy', 'gz'))]
    pallas_call x0 -> x4, Pallas kernels: none -> 45.8 us  [the longest x1 32.5 us: on_device(): pl.pallas_call(first_kernel, name='first', in_specs=[SM, ANY, ANY, VM, VM...]
    ppermute x21 -> x6, starting transfers between devices: 42.9 us -> 8.32 us  [moved_along(): return lax.ppermute(block, axis, [(i, (i + by) % n) for i in range(n)])]
    all_to_all x0 -> x1, blocking collectives: none -> 26.6 us  [on_device(): r = lax.all_to_all(most, AXES, 0, 0, tiled=True)]
    slice x13 -> x0, local copies, waits for them, and re-layouts: 18 us -> none  [the longest x2 7.68 us: on_device(): partial_value[:, 1:-1]]
    ppermute x21 -> x6, waiting for transfers between devices: 26.5 us -> 10.2 us  [moved_along(): return lax.ppermute(block, axis, [(i, (i + by) % n) for i in range(n)])]
    another operation x3 -> x0, local copies, waits for them, and re-layouts: 7.81 us -> none  [spread_block(): stacked = jnp.stack([first, second], axis=position + 1)]
    another operation x8 -> x0, other arithmetic: 5.47 us -> none  [the longest x6 3.14 us: spread_block(): stacked = jnp.stack([first, second], axis=position + 1)]
  transfers between devices with their start and end apart: 21 -> 6, of which waited for: 12 -> 2; matrix products, arithmetic and copies ran while one was open for 5% -> 0% of each run, Pallas kernels for 0% -> 0%
where the time goes in v1:
time: 96.2 us; the launch traced here: 94.6 us
  Pallas kernels  45.8 us (48%)
  blocking collectives  26.6 us (28%)
  waiting for transfers between devices  10.2 us (11%)
  starting transfers between devices  8.32 us (9%)
  local copies, waits for them, and re-layouts  2.92 us (3%)
    pallas_call x1, Pallas kernels, on_device(): pl.pallas_call(first_kernel, name='first', in_specs=[SM, ANY, ANY, VM, VM...  32.5 us
    all_to_all x1, blocking collectives, on_device(): r = lax.all_to_all(most, AXES, 0, 0, tiled=True)  26.6 us
    ppermute x6, waiting for transfers between devices, moved_along(): return lax.ppermute(block, axis, [(i, (i + by) % n) for i in range(n)])  10.2 us
    ppermute x6, starting transfers between devices, moved_along(): return lax.ppermute(block, axis, [(i, (i + by) % n) for i in range(n)])  8.32 us
    pallas_call x1, Pallas kernels, on_device(): pl.pallas_call(last_kernel, name='last', in_specs=[VM] * 11, out_specs=[V...  6.86 us
    pallas_call x1, Pallas kernels, on_device(): pl.pallas_call(third_kernel, name='third', in_specs=[VM] * 10, out_specs=...  3.89 us
    unnamed x12, local copies, waits for them, and re-layouts  2.92 us
    pallas_call x1, Pallas kernels, on_device(): pl.pallas_call(second_kernel, name='second', in_specs=[VM] * 8, out_specs...  2.61 us
  transfers between devices with their start and end apart: 6, of which 2 were waited for; matrix products, arithmetic and copies ran while one was open for 0% of the time, Pallas kernels for 0%

profile of v1, /device:TPU:1, one launch (start us, length us, event | category | flops | bytes accessed | tf_op | source)
XLA Modules:
  0.0 94.6 jit_solution(2097835737818181872)
XLA Ops:
  0.6 32.5 %first.1 = (f32[16,32,256]{2,1,0:T(8,128)}, f32[18,32,256]{2,1,0:T(8,128)}, f32[256,128]{1,0:T(8,128)}, f32[4,16,128]{2,1,0:T(8,128)}) custom-call(f32[4]{0:T(128)} %ratio.1, f32[3,8,32,256]{3,2,1,0:T(8,128)} %d.5, f32[3,8,32,256]{3,2,1,0:T(8,128)} %v.7, f32[4,16,128]{2,1,0:T(8,128)} %rho.5, f32[4,16,128]{2,1,0:T(8,128)} %energy.1, s32[4,16,128]{2,1,0:T(8,128)} %region.1, ...), custom_call_target="tpu_custom_call" | custom-call | tf_op jit(solution)/shard_map/first/pallas_call | solution.py:384
  33.1 3.3 %collective-permute-start.1 = (f32[18,32,256]{2,1,0:T(8,128)}, f32[18,32,256]{2,1,0:T(8,128)S(1)}, u32[]{:S(2)}, u32[]{:S(2)}) collective-permute-start(f32[18,32,256]{2,1,0:T(8,128)} %get-tuple-element.15), channel_id=1, source_target_pairs={{0,192},{64,0},{128,64},{192,128},{1,193},{65,1},{129,65},{193,129... | collective-permute-start | bytes 1769480 | tf_op jit(solution)/shard_map/ppermute | solution.py:379
  36.4 0.0 collective-permute-start
  36.4 26.6 %all_to_all.11 = f32[256,1,128]{2,1,0:T(1,128)} all-to-all(f32[256,1,128]{2,1,0:T(1,128)} %bitcast.7), channel_id=1, replica_groups=mesh['gx'=4,'gy'=16,'gz'=4] {'gx','gy','gz'}, dimensions={0} | all-to-all | bytes 262144 | tf_op jit(solution)/shard_map/all_to_all | solution.py:403
  63.0 0.0 collective-permute-done.low
  63.0 0.0 copy-start.1
  63.0 0.0 collective-permute-done.1.high
  63.0 0.0 copy-start
  63.0 0.8 copy-done.1
  63.8 0.2 copy-done
  64.1 2.6 %second.1 = (f32[88,256]{1,0:T(8,128)}, f32[104,256]{1,0:T(8,128)}) custom-call(f32[256,128]{1,0:T(8,128)} %bitcast.4, f32[3,8,32,256]{3,2,1,0:T(8,128)} %d.5, f32[3,8,32,256]{3,2,1,0:T(8,128)} %v.7, f32[16,32,256]{2,1,0:T(8,128)} %copy-done.1, f32[18,32,256]{2,1,0:T(8,128)} %copy-done, f32[4,16,128]{2,1,0:T(8,128)} %get-tuple-element.16.pressure, ...), custom_call_target="tpu_custom_call" | custom-call | tf_op jit(solution)/shard_map/second/pallas_call | solution.py:404
  66.7 1.1 %collective-permute-start.3 = (f32[104,256]{1,0:T(8,128)}, f32[104,256]{1,0:T(8,128)S(1)}, u32[]{:S(2)}, u32[]{:S(2)}) collective-permute-start(f32[104,256]{1,0:T(8,128)} %get-tuple-element.18), channel_id=1, source_target_pairs={{0,60},{4,0},{8,4},{12,8},{16,12},{20,16},{24,20},{28,24},{32,28},... | collective-permute-start | bytes 319496 | tf_op jit(solution)/shard_map/ppermute | solution.py:379
  67.7 1.3 %collective-permute-start.2 = (f32[88,256]{1,0:T(8,128)}, f32[88,256]{1,0:T(8,128)S(1)}, u32[]{:S(2)}, u32[]{:S(2)}) collective-permute-start(f32[88,256]{1,0:T(8,128)} %get-tuple-element.17), channel_id=1, source_target_pairs={{0,4},{4,8},{8,12},{12,16},{16,20},{20,24},{24,28},{28,32},{32,36}... | collective-permute-start | bytes 270344 | tf_op jit(solution)/shard_map/ppermute | solution.py:379
  69.0 8.5 %collective-permute-done.2.ylow = f32[88,256]{1,0:T(8,128)S(1)} collective-permute-done((f32[88,256]{1,0:T(8,128)}, f32[88,256]{1,0:T(8,128)S(1)}, u32[]{:S(2)}, u32[]{:S(2)}) %collective-permute-start.2) | collective-permute-done | bytes 90144 | tf_op jit(solution)/shard_map/ppermute | solution.py:379
  77.5 0.0 copy-start.3
  77.5 0.0 collective-permute-done.3.yhigh
  77.5 0.6 copy-done.3
  78.2 0.0 copy-start.2
  78.2 0.6 copy-done.2
  78.8 3.9 %third.1 = (f32[39,48,256]{2,1,0:T(8,128)}, f32[16,24,128]{2,1,0:T(8,128)}, f32[2,48,128]{2,1,0:T(8,128)}, f32[2,48,128]{2,1,0:T(8,128)}) custom-call(f32[256,128]{1,0:T(8,128)} %bitcast.5, f32[3,8,32,256]{3,2,1,0:T(8,128)} %d.5, f32[3,8,32,256]{3,2,1,0:T(8,128)} %v.7, f32[16,32,256]{2,1,0:T(8,128)} %copy-done.1, f32[18,32,256]{2,1,0:T(8,128)} %copy-done, ...), custom_call_target="tpu_custom_call" | custom-call | tf_op jit(solution)/shard_map/third/pallas_call | solution.py:413
  82.7 0.4 collective-permute-start.4
  83.1 2.3 %collective-permute-start.5 = (f32[2,48,128]{2,1,0:T(8,128)}, f32[2,48,128]{2,1,0:T(8,128)S(1)}, u32[]{:S(2)}, u32[]{:S(2)}) collective-permute-start(f32[2,48,128]{2,1,0:T(8,128)} %get-tuple-element.22), channel_id=1, source_target_pairs={{0,3},{1,0},{2,1},{3,2},{4,7},{5,4},{6,5},{7,6},{8,11},{9,8},{10,9... | collective-permute-start | bytes 147464 | tf_op jit(solution)/shard_map/ppermute | solution.py:379
  85.4 1.7 %collective-permute-done.4.zlow = f32[2,48,128]{2,1,0:T(8,128)S(1)} collective-permute-done((f32[2,48,128]{2,1,0:T(8,128)}, f32[2,48,128]{2,1,0:T(8,128)S(1)}, u32[]{:S(2)}, u32[]{:S(2)}) %collective-permute-start.4) | collective-permute-done | bytes 49184 | tf_op jit(solution)/shard_map/ppermute | solution.py:379
  87.1 0.0 copy-start.4
  87.1 0.0 collective-permute-done.5.zhigh
  87.1 0.0 copy-start.5
  87.1 0.6 copy-done.4
  87.7 0.0 copy-done.5
  87.7 6.9 %last.1 = (f32[3,8,32,256]{3,2,1,0:T(8,128)}, f32[3,8,32,256]{3,2,1,0:T(8,128)}, f32[4,16,128]{2,1,0:T(8,128)}) custom-call(f32[256,128]{1,0:T(8,128)} %bitcast.6, f32[3,8,32,256]{3,2,1,0:T(8,128)} %v.7, f32[39,48,256]{2,1,0:T(8,128)} %get-tuple-element.19.ext, f32[16,24,128]{2,1,0:T(8,128)} %get-tuple-element.20.zones, f32[4,16,128]{2,1,0:T(8,128)} %tracer.7, ...), custom_call_target="tpu_custom_call" | custom-call | tf_op jit(solution)/shard_map/last/pallas_call | solution.py:428
Async XLA Ops:
  33.1 29.9 %collective-permute-start.1 = (f32[18,32,256]{2,1,0:T(8,128)}, f32[18,32,256]{2,1,0:T(8,128)S(1)}, u32[]{:S(2)}, u32[]{:S(2)}) collective-permute-start(f32[18,32,256]{2,1,0:T(8,128)} %get-tuple-element.15), channel_id=1, source_target_pairs={{0,192},{64,0},{128,64},{192,128},{1,193},{65,1},{129,65},{193,129... | collective-permute-start | bytes 1769480 | tf_op jit(solution)/shard_map/ppermute | solution.py:379
  36.4 26.6 %collective-permute-start = (f32[16,32,256]{2,1,0:T(8,128)}, f32[16,32,256]{2,1,0:T(8,128)S(1)}, u32[]{:S(2)}, u32[]{:S(2)}) collective-permute-start(f32[16,32,256]{2,1,0:T(8,128)} %get-tuple-element.14), channel_id=1, source_target_pairs={{0,64},{64,128},{128,192},{192,0},{1,65},{65,129},{129,193},{193,1... | collective-permute-start | bytes 1572872 | tf_op jit(solution)/shard_map/ppermute | solution.py:379
  63.0 0.8 copy-start.1
  63.0 1.0 %copy-start = (f32[18,32,256]{2,1,0:T(8,128)}, f32[18,32,256]{2,1,0:T(8,128)S(1)}, u32[]{:S(2)}) copy-start(f32[18,32,256]{2,1,0:T(8,128)S(1)} %collective-permute-done.1.high) | copy-start | bytes 1769476
  66.7 10.9 %collective-permute-start.3 = (f32[104,256]{1,0:T(8,128)}, f32[104,256]{1,0:T(8,128)S(1)}, u32[]{:S(2)}, u32[]{:S(2)}) collective-permute-start(f32[104,256]{1,0:T(8,128)} %get-tuple-element.18), channel_id=1, source_target_pairs={{0,60},{4,0},{8,4},{12,8},{16,12},{20,16},{24,20},{28,24},{32,28},... | collective-permute-start | bytes 319496 | tf_op jit(solution)/shard_map/ppermute | solution.py:379
  67.7 9.8 %collective-permute-start.2 = (f32[88,256]{1,0:T(8,128)}, f32[88,256]{1,0:T(8,128)S(1)}, u32[]{:S(2)}, u32[]{:S(2)}) collective-permute-start(f32[88,256]{1,0:T(8,128)} %get-tuple-element.17), channel_id=1, source_target_pairs={{0,4},{4,8},{8,12},{12,16},{16,20},{20,24},{24,28},{28,32},{32,36}... | collective-permute-start | bytes 270344 | tf_op jit(solution)/shard_map/ppermute | solution.py:379
  77.5 0.6 copy-start.3
  78.2 0.6 copy-start.2
  82.7 4.4 %collective-permute-start.4 = (f32[2,48,128]{2,1,0:T(8,128)}, f32[2,48,128]{2,1,0:T(8,128)S(1)}, u32[]{:S(2)}, u32[]{:S(2)}) collective-permute-start(f32[2,48,128]{2,1,0:T(8,128)} %get-tuple-element.21), channel_id=1, source_target_pairs={{0,1},{1,2},{2,3},{3,0},{4,5},{5,6},{6,7},{7,4},{8,9},{9,10},{10,1... | collective-permute-start | bytes 147464 | tf_op jit(solution)/shard_map/ppermute | solution.py:379
  83.1 4.0 %collective-permute-start.5 = (f32[2,48,128]{2,1,0:T(8,128)}, f32[2,48,128]{2,1,0:T(8,128)S(1)}, u32[]{:S(2)}, u32[]{:S(2)}) collective-permute-start(f32[2,48,128]{2,1,0:T(8,128)} %get-tuple-element.22), channel_id=1, source_target_pairs={{0,3},{1,0},{2,1},{3,2},{4,7},{5,4},{6,5},{7,6},{8,11},{9,8},{10,9... | collective-permute-start | bytes 147464 | tf_op jit(solution)/shard_map/ppermute | solution.py:379
  87.1 0.6 copy-start.4
  87.1 0.6 copy-start.5

commit v2 on v1

--- a/solution.py
+++ b/solution.py
@@ -5,10 +5,10 @@
 from jax.experimental.pallas import tpu as pltpu
 from jax.sharding import PartitionSpec as P
 
+
 AXES = ("gx", "gy", "gz")
 VM = pl.BlockSpec(memory_space=pltpu.VMEM)
 SM = pl.BlockSpec(memory_space=pltpu.SMEM)
-ANY = pl.BlockSpec(memory_space=pl.ANY)
 F32 = jnp.float32
 
 NX, NY, NZ = 8, 32, 256
@@ -52,11 +52,15 @@
 
 Y_LOW, Y_LOW_N = row_table(low_rows)
 Y_HIGH, Y_HIGH_N = row_table(high_rows)
+LOW_ZONES, HIGH_ZONES = 2 * Y_LOW_N, 2 * Y_HIGH_N
 EX = 2 * (MX + 4)
-Y_LOW_SIZE = -(-(Y_LOW_N + EX + MX) // 8) * 8
-Y_HIGH_SIZE = -(-(Y_HIGH_N + EX + MX) // 8) * 8
-ZONE_SLOT = NP
-TRACER_SLOT = NP + 2 * (MX + 4)
+Y_LOW_SIZE = -(-(LOW_ZONES + EX + MX) // 8) * 8
+Y_HIGH_SIZE = -(-(HIGH_ZONES + EX + MX) // 8) * 8
+Z_PLANES = [(c, x) for c, x in PLANES if -2 <= x <= NX + (2 if c == 0 else 1)]
+ZN = len(Z_PLANES)
+ZONE_SLOT = 2 * ZN
+TRACER_SLOT = ZONE_SLOT + 2 * (MX + 4)
+Z_TILES = -(-(TRACER_SLOT + MX) // 32)
 
 
 def step_of(r):
@@ -64,23 +68,11 @@
     return 0.5 / jnp.sqrt(top)
 
 
-def first_kernel(ratio, d, v, rho, energy, region, tracer, low, high, most, pressure, zl, zh, sems):
-    copies = []
-
-    def copy(src, dst):
-        cp = pltpu.make_async_copy(src, dst, sems.at[len(copies)])
-        cp.start()
-        copies.append(cp)
-
-    at = 0
+def first_kernel(ratio, d, v, rho, energy, region, tracer, low, high, most, pressure):
     for f, array in enumerate((d, v)):
-        for c in range(3):
-            n = 3 if c == 0 else 2
-            off = f * NL + X_LOW.index((c, -n))
-            copy(array.at[c, pl.ds(NX - n, n)], low.at[pl.ds(off, n)])
-            n = 4 if c == 0 else 2
-            off = f * NH + X_HIGH.index((c, NX))
-            copy(array.at[c, pl.ds(0, n)], high.at[pl.ds(off, n)])
+        for table, size, out, shift in ((X_LOW, NL, low, NX), (X_HIGH, NH, high, -NX)):
+            for at, (c, x) in enumerate(table):
+                out[f * size + at] = array[c, x + shift]
     top = jnp.zeros((MY, MZ), F32)
     for i in range(MX):
         reg = region[i]
@@ -92,20 +84,14 @@
         pr = (zone_ratio - 1.0) * rho[i] * energy[i]
         pressure[i] = pr
         top = jnp.maximum(top, zone_ratio * (zone_ratio - 1.0) * energy[i])
-        if i < 2:
-            zh[0, :MY, i * MZ : (i + 1) * MZ] = pr
-            zh[0, MY:, i * MZ : (i + 1) * MZ] = rho[i]
-        else:
-            zl[0, :MY, (i - 2) * MZ : (i - 1) * MZ] = pr
-            zl[0, MY:, (i - 2) * MZ : (i - 1) * MZ] = rho[i]
-    zh[1, :MY, :MZ] = tracer[0]
-    zl[1, :MY, :MZ] = tracer[MX - 1]
-    copy(zl, low.at[pl.ds(2 * NL, 2)])
-    copy(zh, high.at[pl.ds(2 * NH, 2)])
+        out, at = (high, 2 * NH) if i < 2 else (low, 2 * NL)
+        lanes = slice(i % 2 * MZ, (i % 2 + 1) * MZ)
+        out[at, :MY, lanes] = pr
+        out[at, MY:, lanes] = rho[i]
+    high[2 * NH + 1, :MY, :MZ] = tracer[0]
+    low[2 * NL + 1, :MY, :MZ] = tracer[MX - 1]
     top = jnp.max(jnp.max(top, axis=0, keepdims=True), axis=1, keepdims=True)
     most[...] = jnp.broadcast_to(top, most.shape)
-    for cp in copies:
-        cp.wait()
 
 
 def zone_plane(i, own, low, high, which):
@@ -127,14 +113,13 @@
     return high.at[i], high.at[NH + i]
 
 
-def second_kernel(r, d, v, low, high, pressure, rho, tracer, ylow, yhigh):
-    step = step_of(r)
-    for table, out, start, stop in ((Y_LOW, ylow, None, NY), (Y_HIGH, yhigh, 0, None)):
+def second_kernel(d, v, low, high, pressure, rho, tracer, ylow, yhigh):
+    for table, size, out, top in ((Y_LOW, Y_LOW_N, ylow, True), (Y_HIGH, Y_HIGH_N, yhigh, False)):
         for c, x, at, n in table:
-            first = NY - n if start is None else 0
-            a, b = node_pair(c, x, d, v, low, high)
-            out[pl.ds(at, n), :] = a[pl.ds(first, n), :] + step * b[pl.ds(first, n), :]
-    for out, base, first, edge in ((ylow, Y_LOW_N, MY - 2, MY - 1), (yhigh, Y_HIGH_N, 0, 0)):
+            first = NY - n if top else 0
+            for f, plane in enumerate(node_pair(c, x, d, v, low, high)):
+                out[pl.ds(f * size + at, n), :] = plane[pl.ds(first, n), :]
+    for out, base, first, edge in ((ylow, LOW_ZONES, MY - 2, MY - 1), (yhigh, HIGH_ZONES, 0, 0)):
         for i in range(-2, MX + 2):
             for which in range(2):
                 lanes = slice(which * MZ, (which + 1) * MZ)
@@ -145,48 +130,53 @@
             out[pl.ds(base + EX + i, 1), :MZ] = tracer[i, pl.ds(edge, 1), :]
 
 
-def third_kernel(
-    r, d, v, low, high, pressure, rho, tracer, ylow, yhigh, ext, zones, zlow, zhigh
-):
-    step = step_of(r)
-    lows = {(c, x): (at, n) for c, x, at, n in Y_LOW}
-    highs = {(c, x): (at, n) for c, x, at, n in Y_HIGH}
-    for e, (c, x) in enumerate(PLANES):
-        a, b = node_pair(c, x, d, v, low, high)
-        ext[e, pl.ds(8, NY), :] = a[...] + step * b[...]
-        if (c, x) in lows:
-            at, n = lows[c, x]
-            ext[e, pl.ds(8 - n, n), :] = ylow[pl.ds(at, n), :]
-        if (c, x) in highs:
-            at, n = highs[c, x]
-            ext[e, pl.ds(8 + NY, n), :] = yhigh[pl.ds(at, n), :]
+LOW_AT = {(c, x): (at, n) for c, x, at, n in Y_LOW}
+HIGH_AT = {(c, x): (at, n) for c, x, at, n in Y_HIGH}
+
+
+def zone_block(zones, pressure, rho, low, high, ylow, yhigh):
     for which in range(2):
         lanes = slice(which * MZ, (which + 1) * MZ)
         for i in range(-2, MX + 2):
             k = which * (MX + 4) + i + 2
-            zones[k, pl.ds(4, MY), :] = zone_plane(i, (pressure, rho), low, high, which)
-            zones[k, pl.ds(2, 2), :] = ylow[pl.ds(Y_LOW_N + 2 * (i + 2), 2), lanes]
-            zones[k, pl.ds(4 + MY, 2), :] = yhigh[pl.ds(Y_HIGH_N + 2 * (i + 2), 2), lanes]
+            zones[k, pl.ds(4, MY), :MZ] = zone_plane(i, (pressure, rho), low, high, which)
+            zones[k, pl.ds(2, 2), :MZ] = ylow[pl.ds(LOW_ZONES + 2 * (i + 2), 2), lanes]
+            zones[k, pl.ds(4 + MY, 2), :MZ] = yhigh[pl.ds(HIGH_ZONES + 2 * (i + 2), 2), lanes]
+
+
+def third_kernel(
+    d, v, low, high, pressure, rho, tracer, ylow, yhigh, zlow, zhigh, zones, lefts, rights
+):
+    zone_block(zones, pressure, rho, low, high, ylow, yhigh)
     lane = lax.broadcasted_iota(jnp.int32, (1, 128), 1)
-    for tile in range(2):
+    for tile in range(Z_TILES):
         zlow[tile] = jnp.zeros((48, 128), F32)
         zhigh[tile] = jnp.zeros((48, 128), F32)
-        for s in range(32):
-            slot = tile * 32 + s
-            if slot >= TRACER_SLOT + MX:
-                break
-            if slot < ZONE_SLOT:
-                left, right, n = ext[slot, :, :128], ext[slot, :, 128:], 48
-            elif slot < TRACER_SLOT:
-                left = right = zones[slot - ZONE_SLOT]
-                n = 24
-            else:
-                left = right = tracer[slot - TRACER_SLOT]
-                n = MY
-            here = (lane >= 4 * s) & (lane < 4 * s + 4)
-            rows = pl.ds(0, n)
+    for slot in range(TRACER_SLOT + MX):
+        tile, s = divmod(slot, 32)
+        here = (lane >= 4 * s) & (lane < 4 * s + 4)
+
+        def put(rows, left, right):
             zhigh[tile, rows] = jnp.where(here, roll(left, 4 * s, 1), zhigh[tile, rows])
             zlow[tile, rows] = jnp.where(here, roll(right, 4 * s + 4, 1), zlow[tile, rows])
+
+        if slot < ZONE_SLOT:
+            f, e = divmod(slot, ZN)
+            c, x = Z_PLANES[e]
+            plane = node_pair(c, x, d, v, low, high)[f]
+            put(pl.ds(8, NY), plane[:, :128], plane[:, 128:])
+            if (c, x) in LOW_AT:
+                at, n = LOW_AT[c, x]
+                lefts[pl.ds(8 - n, n), :] = ylow[pl.ds(f * Y_LOW_N + at, n), :]
+                put(pl.ds(0, 8), lefts[:, :128], lefts[:, 128:])
+            if (c, x) in HIGH_AT:
+                at, n = HIGH_AT[c, x]
+                rights[pl.ds(0, n), :] = yhigh[pl.ds(f * Y_HIGH_N + at, n), :]
+                put(pl.ds(8 + NY, 8), rights[:, :128], rights[:, 128:])
+        elif slot < TRACER_SLOT:
+            put(pl.ds(0, 24), zones[slot - ZONE_SLOT], zones[slot - ZONE_SLOT])
+        else:
+            put(pl.ds(0, MY), tracer[slot - TRACER_SLOT], tracer[slot - TRACER_SLOT])
 
 
 def roll(value, by, axis):
@@ -210,7 +200,7 @@
 
 
 def last_kernel(
-    r, v, ext, zones, tracer, low, high, ylow, yhigh, zlow, zhigh,
+    r, d, v, low, high, pressure, rho, tracer, ylow, yhigh, zlow, zhigh,
     velocity, relaxed, remapped,
     moved, once, pz, qx, qy, qz, qm, moves, gathered, result, tz,
 ):
@@ -224,8 +214,8 @@
         before = roll(zlow[tile, rows], 124 - 4 * s, 1)
         return jnp.where(lane < 4, after, jnp.where(lane >= 124, before, fill))
 
+    zone_block(pz, pressure, rho, low, high, ylow, yhigh)
     for k in range(2 * (MX + 4)):
-        pz[k, :, :MZ] = zones[k]
         pz[k, :, MZ:] = beside(ZONE_SLOT + k, 24, 0.0 if k < MX + 4 else 1.0)
     k = lax.broadcasted_iota(jnp.int32, (2 * MZ, 384), 0)
     n = lax.broadcasted_iota(jnp.int32, (2 * MZ, 384), 1)
@@ -271,18 +261,29 @@
                 q = qy if c == 1 else qz
                 force = whole(q, i)
                 force = force + whole(q, i - 1) if x % 2 == 0 else 4.0 * force
-            third = beside(e, 48, 0.0)
-            if force is None:
-                moved[e, :, :NZ] = ext[e]
-                moved[e, :, NZ:] = third
-                if 0 <= x < NX:
-                    velocity[c, x] = v[c, x]
+            here, there = node_pair(c, x, d, v, low, high)
+            moved[e, pl.ds(8, NY), :NZ] = here[...] + step * there[...]
+            if (c, x) in LOW_AT:
+                at, n = LOW_AT[c, x]
+                moved[e, pl.ds(8 - n, n), :NZ] = (
+                    ylow[pl.ds(at, n), :] + step * ylow[pl.ds(Y_LOW_N + at, n), :]
+                )
+            if (c, x) in HIGH_AT:
+                at, n = HIGH_AT[c, x]
+                moved[e, pl.ds(8 + NY, n), :NZ] = (
+                    yhigh[pl.ds(at, n), :] + step * yhigh[pl.ds(Y_HIGH_N + at, n), :]
+                )
+            if (c, x) in Z_PLANES:
+                z = Z_PLANES.index((c, x))
+                moved[e, :, NZ:] = beside(z, 48, 0.0) + step * beside(ZN + z, 48, 0.0)
             else:
+                moved[e, :, NZ:] = jnp.zeros((48, 128), F32)
+            if force is not None:
                 gain = force * push
-                moved[e, :, :NZ] = ext[e] + step * gain[:, :NZ]
-                moved[e, :, NZ:] = third + step * gain[:, NZ:]
-                if 0 <= x < NX:
-                    velocity[c, x] = v[c, x] + gain[8 : 8 + NY, :NZ]
+                moved[e] = moved[e] + step * gain
+            if 0 <= x < NX:
+                new = v[c, x]
+                velocity[c, x] = new if force is None else new + gain[8 : 8 + NY, :NZ]
 
     def sweep(ref, e):
         now = ref[e]
@@ -326,8 +327,8 @@
     for i in range(MX):
         now = tracer[i]
         tz[pl.ds(8, MY), :] = now
-        tz[pl.ds(7, 1), :] = ylow[pl.ds(Y_LOW_N + EX + i, 1), :MZ]
-        tz[pl.ds(8 + MY, 1), :] = yhigh[pl.ds(Y_HIGH_N + EX + i, 1), :MZ]
+        tz[pl.ds(7, 1), :] = ylow[pl.ds(LOW_ZONES + EX + i, 1), :MZ]
+        tz[pl.ds(8 + MY, 1), :] = yhigh[pl.ds(HIGH_ZONES + EX + i, 1), :MZ]
         side = beside(TRACER_SLOT + i, MY, 0.0)
         edge = result[pl.ds(z0 + 16 * i, 16), MZ:]
         middle = result[pl.ds(z0 + 16 * i, 16), :MZ]
@@ -374,61 +375,75 @@
     return jax.ShapeDtypeStruct(dims, F32)
 
 
+def local_of(*dims):
+    return pltpu.VMEM(dims, F32)
+
+
+def on_chip(array):
+    return pltpu.with_memory_space_constraint(array, pltpu.VMEM)
+
+
 def moved_along(block, axis, by):
     n = lax.axis_size(axis)
-    return lax.ppermute(block, axis, [(i, (i + by) % n) for i in range(n)])
+    return on_chip(lax.ppermute(block, axis, [(i, (i + by) % n) for i in range(n)]))
+
+
+def pack_y(*operands):
+    return pl.pallas_call(
+        second_kernel,
+        name="second",
+        compiler_params=pltpu.CompilerParams(vmem_limit_bytes=8 << 20),
+        in_specs=[VM] * 7,
+        out_specs=[VM] * 2,
+        out_shape=[local_of(Y_LOW_SIZE, NZ), local_of(Y_HIGH_SIZE, NZ)],
+    )(*operands)
 
 
 def on_device(displacement, velocity, density, energy, region, heat_ratio, tracer):
     n_devices = lax.axis_size(AXES)
+    displacement, velocity, density, energy, region, tracer = (
+        on_chip(array) for array in (displacement, velocity, density, energy, region, tracer)
+    )
     low, high, most, pressure = pl.pallas_call(
         first_kernel,
         name="first",
-        in_specs=[SM, ANY, ANY, VM, VM, VM, VM],
-        out_specs=[ANY, ANY, VM, VM],
+        compiler_params=pltpu.CompilerParams(vmem_limit_bytes=8 << 20),
+        in_specs=[SM] + [VM] * 6,
+        out_specs=[VM] * 4,
         out_shape=[
-            shape_of(2 * NL + 2, NY, NZ),
-            shape_of(2 * NH + 2, NY, NZ),
-            shape_of(n_devices, 128),
-            shape_of(MX, MY, MZ),
-        ],
-        scratch_shapes=[
-            pltpu.VMEM((2, NY, NZ), F32),
-            pltpu.VMEM((2, NY, NZ), F32),
-            pltpu.SemaphoreType.DMA((14,)),
+            local_of(2 * NL + 2, NY, NZ),
+            local_of(2 * NH + 2, NY, NZ),
+            local_of(n_devices, 128),
+            local_of(MX, MY, MZ),
         ],
     )(heat_ratio, displacement, velocity, density, energy, region, tracer)
     low = moved_along(low, "gx", 1)
     high = moved_along(high, "gx", -1)
-    r = lax.all_to_all(most, AXES, 0, 0, tiled=True)
-    ylow, yhigh = pl.pallas_call(
-        second_kernel,
-        name="second",
-        in_specs=[VM] * 8,
-        out_specs=[VM] * 2,
-        out_shape=[shape_of(Y_LOW_SIZE, NZ), shape_of(Y_HIGH_SIZE, NZ)],
-    )(r, displacement, velocity, low, high, pressure, density, tracer)
+    r = on_chip(lax.all_to_all(most, AXES, 0, 0, tiled=True))
+    ylow, yhigh = pack_y(displacement, velocity, low, high, pressure, density, tracer)
     ylow = moved_along(ylow, "gy", 1)
     yhigh = moved_along(yhigh, "gy", -1)
-    ext, zones, zlow, zhigh = pl.pallas_call(
+    zlow, zhigh = pl.pallas_call(
         third_kernel,
         name="third",
-        in_specs=[VM] * 10,
-        out_specs=[VM] * 4,
-        out_shape=[
-            shape_of(NP, 48, NZ),
-            shape_of(2 * (MX + 4), 24, MZ),
-            shape_of(2, 48, 128),
-            shape_of(2, 48, 128),
+        compiler_params=pltpu.CompilerParams(vmem_limit_bytes=8 << 20),
+        in_specs=[VM] * 9,
+        out_specs=[VM] * 2,
+        out_shape=[local_of(Z_TILES, 48, 128)] * 2,
+        scratch_shapes=[
+            pltpu.VMEM((2 * (MX + 4), 24, MZ), F32),
+            pltpu.VMEM((8, NZ), F32),
+            pltpu.VMEM((8, NZ), F32),
         ],
-    )(r, displacement, velocity, low, high, pressure, density, tracer, ylow, yhigh)
+    )(displacement, velocity, low, high, pressure, density, tracer, ylow, yhigh)
     zlow = moved_along(zlow, "gz", 1)
     zhigh = moved_along(zhigh, "gz", -1)
     q = pltpu.VMEM((3 * (MX + 4), 48, 128), F32)
     return pl.pallas_call(
         last_kernel,
         name="last",
-        in_specs=[VM] * 11,
+        compiler_params=pltpu.CompilerParams(vmem_limit_bytes=30 << 20),
+        in_specs=[VM] * 12,
         out_specs=[VM] * 3,
         out_shape=[shape_of(3, NX, NY, NZ), shape_of(3, NX, NY, NZ), shape_of(MX, MY, MZ)],
         scratch_shapes=[
@@ -441,7 +456,9 @@
             pltpu.VMEM((256, 2 * MZ), F32),
             pltpu.VMEM((MY + 16, MZ), F32),
         ],
-    )(r, velocity, ext, zones, tracer, low, high, ylow, yhigh, zlow, zhigh)
+    )(
+        r, displacement, velocity, low, high, pressure, density, tracer, ylow, yhigh, zlow, zhigh
+    )
 
 
 def solution(mesh):

time: 96.2 us -> 67.4 us (0.70)
  the two profiles are of different devices: /device:TPU:1 before, /device:TPU:32 now
where the time goes in v2:
time: 67.4 us; the launch traced here: 66.9 us
  waiting for transfers between devices  29 us (43%)
  starting transfers between devices  22.2 us (33%)
  Pallas kernels  8.33 us (12%)
  local copies, waits for them, and re-layouts  6.62 us (10%)
  between operations  0.7 us (1%)
    ppermute x6, waiting for transfers between devices, moved_along(): lax.ppermute(block, axis, [(i, (i + by) % n) for i in range(n)])  29 us
    ppermute x6, starting transfers between devices, moved_along(): lax.ppermute(block, axis, [(i, (i + by) % n) for i in range(n)])  14.8 us
    all_to_all x1, starting transfers between devices, on_device(): r = on_chip(lax.all_to_all(most, AXES, 0, 0, tiled=True))  7.36 us
    unnamed x24, local copies, waits for them, and re-layouts  6.62 us
    pallas_call x1, Pallas kernels, on_device(): pl.pallas_call(last_kernel, name='last', compiler_params=pltpu.CompilerPa...  5.63 us
    pallas_call x1, Pallas kernels, on_device(): pl.pallas_call(first_kernel, name='first', compiler_params=pltpu.Compiler...  1.36 us
  transfers between devices with their start and end apart: 7, of which 4 were waited for; matrix products, arithmetic and copies ran while one was open for 0% of the time, Pallas kernels for 2%

profile of v2, /device:TPU:32, one launch (start us, length us, event | category | flops | bytes accessed | tf_op | source)
XLA Modules:
  0.0 66.9 jit_solution(7142474807120634575)
XLA Ops:
  0.6 0.0 copy-start
  0.6 1.1 %copy-done = f32[3,8,32,256]{3,2,1,0:T(8,128)S(1)} copy-done((f32[3,8,32,256]{3,2,1,0:T(8,128)S(1)}, f32[3,8,32,256]{3,2,1,0:T(8,128)}, u32[]{:S(2)}) %copy-start) | copy-done | bytes 786456
  1.8 0.0 copy-start.2
  1.8 1.1 %copy-done.2 = f32[3,8,32,256]{3,2,1,0:T(8,128)S(1)} copy-done((f32[3,8,32,256]{3,2,1,0:T(8,128)S(1)}, f32[3,8,32,256]{3,2,1,0:T(8,128)}, u32[]{:S(2)}) %copy-start.2) | copy-done | bytes 786456
  2.9 0.0 copy-start.4
  2.9 0.8 %copy-done.4 = f32[4,16,128]{2,1,0:T(8,128)S(1)} copy-done((f32[4,16,128]{2,1,0:T(8,128)S(1)}, f32[4,16,128]{2,1,0:T(8,128)}, u32[]{:S(2)}) %copy-start.4) | copy-done | bytes 32792
  3.7 0.0 copy-start.6
  3.7 0.8 %copy-done.6 = f32[4,16,128]{2,1,0:T(8,128)S(1)} copy-done((f32[4,16,128]{2,1,0:T(8,128)S(1)}, f32[4,16,128]{2,1,0:T(8,128)}, u32[]{:S(2)}) %copy-start.6) | copy-done | bytes 32792
  4.4 0.0 copy-start.8
  4.4 0.8 %copy-done.8 = f32[4,16,128]{2,1,0:T(8,128)S(1)} copy-done((f32[4,16,128]{2,1,0:T(8,128)S(1)}, f32[4,16,128]{2,1,0:T(8,128)}, u32[]{:S(2)}) %copy-start.8) | copy-done | bytes 32792
  5.2 0.0 copy-start.9
  5.2 0.8 %copy-done.9 = s32[4,16,128]{2,1,0:T(8,128)S(1)} copy-done((s32[4,16,128]{2,1,0:T(8,128)S(1)}, s32[4,16,128]{2,1,0:T(8,128)}, u32[]{:S(2)}) %copy-start.9) | copy-done | bytes 32792
  5.9 0.0 copy-start.10
  5.9 0.7 copy-done.10
  6.6 0.0 copy-start.1
  6.6 0.0 copy-start.3
  6.6 0.0 copy-start.5
  6.6 1.4 %first.1 = (f32[16,32,256]{2,1,0:T(8,128)S(1)}, f32[18,32,256]{2,1,0:T(8,128)S(1)}, f32[256,128]{1,0:T(8,128)}, f32[4,16,128]{2,1,0:T(8,128)S(1)}) custom-call(f32[4]{0:T(128)S(1)} %copy-done.10, f32[3,8,32,256]{3,2,1,0:T(8,128)S(1)} %copy-done, f32[3,8,32,256]{3,2,1,0:T(8,128)S(1)} %copy-done.2, f32[4,16,128]{2,1,0:T(8,128)S(1)} %copy-done.4, ...), custom_call_target="tpu_custom_call" | custom-call | tf_op jit(solution)/shard_map/first/pallas_call | solution.py:407
  8.0 0.0 collective-permute-start.1
  8.0 0.5 collective-permute-start
  8.5 13.7 %collective-permute-done.low = f32[16,32,256]{2,1,0:T(8,128)S(1)} collective-permute-done((f32[16,32,256]{2,1,0:T(8,128)S(1)}, f32[16,32,256]{2,1,0:T(8,128)S(1)}, u32[]{:S(2)}, u32[]{:S(2)}) %collective-permute-start) | collective-permute-done | bytes 524320 | tf_op jit(solution)/shard_map/ppermute | solution.py:388
  22.2 0.0 collective-permute-done.1.high
  22.2 0.0 copy-done.1
  22.2 0.0 copy-done.3
  22.2 0.0 copy-done.5
  22.2 0.1 second.1
  22.4 0.0 copy-start.11
  22.4 0.7 copy-done.11
  23.0 8.0 %collective-permute-start.3 = (f32[184,256]{1,0:T(8,128)S(1)}, f32[184,256]{1,0:T(8,128)S(1)}, u32[]{:S(2)}, u32[]{:S(2)}) collective-permute-start(f32[184,256]{1,0:T(8,128)S(1)} %get-tuple-element.16), channel_id=1, source_target_pairs={{0,60},{4,0},{8,4},{12,8},{16,12},{20,16},{24,20},{28,24},{32,28},... | collective-permute-start | bytes 565256 | tf_op jit(solution)/shard_map/ppermute | solution.py:388
  31.0 0.0 copy-start.7
  31.1 7.4 %all-to-all-start = ((f32[256,1,128]{2,1,0:T(1,128)}), f32[256,1,128]{2,1,0:T(1,128)S(1)}, u32[]{:S(2)}, u32[]{:S(2)}) async-start(f32[256,1,128]{2,1,0:T(1,128)} %bitcast.1), calls=%async_computation | async-start | bytes 262144 | tf_op jit(solution)/shard_map/all_to_all | solution.py:422
  38.4 3.0 %collective-permute-start.2 = (f32[152,256]{1,0:T(8,128)}, f32[152,256]{1,0:T(8,128)S(1)}, u32[]{:S(2)}, u32[]{:S(2)}) collective-permute-start(f32[152,256]{1,0:T(8,128)} %copy-done.11), channel_id=1, source_target_pairs={{0,4},{4,8},{8,12},{12,16},{16,20},{20,24},{24,28},{28,32},{32,36}... | collective-permute-start | bytes 466952 | tf_op jit(solution)/shard_map/ppermute | solution.py:388
  41.4 12.7 %collective-permute-done.2.ylow = f32[152,256]{1,0:T(8,128)S(1)} collective-permute-done((f32[152,256]{1,0:T(8,128)}, f32[152,256]{1,0:T(8,128)S(1)}, u32[]{:S(2)}, u32[]{:S(2)}) %collective-permute-start.2) | collective-permute-done | bytes 155680 | tf_op jit(solution)/shard_map/ppermute | solution.py:388
  54.1 0.0 collective-permute-done.3.yhigh
  54.1 0.0 copy-done.7
  54.1 1.2 %third.1 = (f32[3,48,128]{2,1,0:T(8,128)S(1)}, f32[3,48,128]{2,1,0:T(8,128)S(1)}) custom-call(f32[3,8,32,256]{3,2,1,0:T(8,128)S(1)} %copy-done.1, f32[3,8,32,256]{3,2,1,0:T(8,128)S(1)} %copy-done.3, f32[16,32,256]{2,1,0:T(8,128)S(1)} %collective-permute-done.low, f32[18,32,256]{2,1,0:T(8,128)S(1)} %collective-permute-done.1.high, ...), custom_call_target="tpu_custom_call" | custom-call | tf_op jit(solution)/shard_map/third/pallas_call | solution.py:426
  55.3 1.6 %collective-permute-start.4 = (f32[3,48,128]{2,1,0:T(8,128)S(1)}, f32[3,48,128]{2,1,0:T(8,128)S(1)}, u32[]{:S(2)}, u32[]{:S(2)}) collective-permute-start(f32[3,48,128]{2,1,0:T(8,128)S(1)} %get-tuple-element.17), channel_id=1, source_target_pairs={{0,1},{1,2},{2,3},{3,0},{4,5},{5,6},{6,7},{7,4},{8,9},{9,10},{10,1... | collective-permute-start | bytes 221192 | tf_op jit(solution)/shard_map/ppermute | solution.py:388
  56.9 1.7 %collective-permute-start.5 = (f32[3,48,128]{2,1,0:T(8,128)S(1)}, f32[3,48,128]{2,1,0:T(8,128)S(1)}, u32[]{:S(2)}, u32[]{:S(2)}) collective-permute-start(f32[3,48,128]{2,1,0:T(8,128)S(1)} %get-tuple-element.18), channel_id=1, source_target_pairs={{0,3},{1,0},{2,1},{3,2},{4,7},{5,4},{6,5},{7,6},{8,11},{9,8},{10,9... | collective-permute-start | bytes 221192 | tf_op jit(solution)/shard_map/ppermute | solution.py:388
  58.6 0.0 all-to-all-done
  58.6 2.3 %collective-permute-done.4.zlow = f32[3,48,128]{2,1,0:T(8,128)S(1)} collective-permute-done((f32[3,48,128]{2,1,0:T(8,128)S(1)}, f32[3,48,128]{2,1,0:T(8,128)S(1)}, u32[]{:S(2)}, u32[]{:S(2)}) %collective-permute-start.4) | collective-permute-done | bytes 73760 | tf_op jit(solution)/shard_map/ppermute | solution.py:388
  60.9 0.3 collective-permute-done.5.zhigh
  61.2 5.6 %last.1 = (f32[3,8,32,256]{3,2,1,0:T(8,128)}, f32[3,8,32,256]{3,2,1,0:T(8,128)}, f32[4,16,128]{2,1,0:T(8,128)}) custom-call(f32[256,128]{1,0:T(8,128)S(1)} %bitcast.4, f32[3,8,32,256]{3,2,1,0:T(8,128)S(1)} %copy-done.1, f32[3,8,32,256]{3,2,1,0:T(8,128)S(1)} %copy-done.3, f32[16,32,256]{2,1,0:T(8,128)S(1)} %collective-permute-done.low, ...), custom_call_target="tpu_custom_call" | custom-call | tf_op jit(solution)/shard_map/last/pallas_call | solution.py:442
Async XLA Ops:
  0.6 1.1 %copy-start = (f32[3,8,32,256]{3,2,1,0:T(8,128)S(1)}, f32[3,8,32,256]{3,2,1,0:T(8,128)}, u32[]{:S(2)}) copy-start(f32[3,8,32,256]{3,2,1,0:T(8,128)} %d.7) | copy-start | bytes 2359300
  1.8 1.1 %copy-start.2 = (f32[3,8,32,256]{3,2,1,0:T(8,128)S(1)}, f32[3,8,32,256]{3,2,1,0:T(8,128)}, u32[]{:S(2)}) copy-start(f32[3,8,32,256]{3,2,1,0:T(8,128)} %v.7) | copy-start | bytes 2359300
  2.9 0.8 %copy-start.4 = (f32[4,16,128]{2,1,0:T(8,128)S(1)}, f32[4,16,128]{2,1,0:T(8,128)}, u32[]{:S(2)}) copy-start(f32[4,16,128]{2,1,0:T(8,128)} %rho.7) | copy-start | bytes 98308
  3.7 0.8 %copy-start.6 = (f32[4,16,128]{2,1,0:T(8,128)S(1)}, f32[4,16,128]{2,1,0:T(8,128)}, u32[]{:S(2)}) copy-start(f32[4,16,128]{2,1,0:T(8,128)} %tracer.7) | copy-start | bytes 98308
  4.4 0.8 %copy-start.8 = (f32[4,16,128]{2,1,0:T(8,128)S(1)}, f32[4,16,128]{2,1,0:T(8,128)}, u32[]{:S(2)}) copy-start(f32[4,16,128]{2,1,0:T(8,128)} %energy.1) | copy-start | bytes 98308
  5.2 0.8 %copy-start.9 = (s32[4,16,128]{2,1,0:T(8,128)S(1)}, s32[4,16,128]{2,1,0:T(8,128)}, u32[]{:S(2)}) copy-start(s32[4,16,128]{2,1,0:T(8,128)} %region.1) | copy-start | bytes 98308
  5.9 0.7 copy-start.10
  6.6 15.6 %copy-start.1 = (f32[3,8,32,256]{3,2,1,0:T(8,128)S(1)}, f32[3,8,32,256]{3,2,1,0:T(8,128)}, u32[]{:S(2)}) copy-start(f32[3,8,32,256]{3,2,1,0:T(8,128)} %d.7) | copy-start | bytes 2359300
  6.6 15.6 %copy-start.3 = (f32[3,8,32,256]{3,2,1,0:T(8,128)S(1)}, f32[3,8,32,256]{3,2,1,0:T(8,128)}, u32[]{:S(2)}) copy-start(f32[3,8,32,256]{3,2,1,0:T(8,128)} %v.7) | copy-start | bytes 2359300
  6.6 15.6 %copy-start.5 = (f32[4,16,128]{2,1,0:T(8,128)S(1)}, f32[4,16,128]{2,1,0:T(8,128)}, u32[]{:S(2)}) copy-start(f32[4,16,128]{2,1,0:T(8,128)} %rho.7) | copy-start | bytes 98308
  8.0 14.2 %collective-permute-start.1 = (f32[18,32,256]{2,1,0:T(8,128)S(1)}, f32[18,32,256]{2,1,0:T(8,128)S(1)}, u32[]{:S(2)}, u32[]{:S(2)}) collective-permute-start(f32[18,32,256]{2,1,0:T(8,128)S(1)} %get-tuple-element.13), channel_id=1, source_target_pairs={{0,192},{64,0},{128,64},{192,128},{1,193},{65,1},{129,65},{193,129... | collective-permute-start | bytes 1769480 | tf_op jit(solution)/shard_map/ppermute | solution.py:388
  8.0 14.2 %collective-permute-start = (f32[16,32,256]{2,1,0:T(8,128)S(1)}, f32[16,32,256]{2,1,0:T(8,128)S(1)}, u32[]{:S(2)}, u32[]{:S(2)}) collective-permute-start(f32[16,32,256]{2,1,0:T(8,128)S(1)} %get-tuple-element.12), channel_id=1, source_target_pairs={{0,64},{64,128},{128,192},{192,0},{1,65},{65,129},{129,193},{193,1... | collective-permute-start | bytes 1572872 | tf_op jit(solution)/shard_map/ppermute | solution.py:388
  22.4 0.7 copy-start.11
  23.0 31.0 %collective-permute-start.3 = (f32[184,256]{1,0:T(8,128)S(1)}, f32[184,256]{1,0:T(8,128)S(1)}, u32[]{:S(2)}, u32[]{:S(2)}) collective-permute-start(f32[184,256]{1,0:T(8,128)S(1)} %get-tuple-element.16), channel_id=1, source_target_pairs={{0,60},{4,0},{8,4},{12,8},{16,12},{20,16},{24,20},{28,24},{32,28},... | collective-permute-start | bytes 565256 | tf_op jit(solution)/shard_map/ppermute | solution.py:388
  31.0 23.0 %copy-start.7 = (f32[4,16,128]{2,1,0:T(8,128)S(1)}, f32[4,16,128]{2,1,0:T(8,128)}, u32[]{:S(2)}) copy-start(f32[4,16,128]{2,1,0:T(8,128)} %tracer.7) | copy-start | bytes 98308
  31.1 27.5 %all-to-all-start = ((f32[256,1,128]{2,1,0:T(1,128)}), f32[256,1,128]{2,1,0:T(1,128)S(1)}, u32[]{:S(2)}, u32[]{:S(2)}) async-start(f32[256,1,128]{2,1,0:T(1,128)} %bitcast.1), calls=%async_computation | async-start | bytes 262144 | tf_op jit(solution)/shard_map/all_to_all | solution.py:422
  38.4 15.6 %collective-permute-start.2 = (f32[152,256]{1,0:T(8,128)}, f32[152,256]{1,0:T(8,128)S(1)}, u32[]{:S(2)}, u32[]{:S(2)}) collective-permute-start(f32[152,256]{1,0:T(8,128)} %copy-done.11), channel_id=1, source_target_pairs={{0,4},{4,8},{8,12},{12,16},{16,20},{20,24},{24,28},{28,32},{32,36}... | collective-permute-start | bytes 466952 | tf_op jit(solution)/shard_map/ppermute | solution.py:388
  55.3 5.6 %collective-permute-start.4 = (f32[3,48,128]{2,1,0:T(8,128)S(1)}, f32[3,48,128]{2,1,0:T(8,128)S(1)}, u32[]{:S(2)}, u32[]{:S(2)}) collective-permute-start(f32[3,48,128]{2,1,0:T(8,128)S(1)} %get-tuple-element.17), channel_id=1, source_target_pairs={{0,1},{1,2},{2,3},{3,0},{4,5},{5,6},{6,7},{7,4},{8,9},{9,10},{10,1... | collective-permute-start | bytes 221192 | tf_op jit(solution)/shard_map/ppermute | solution.py:388
  56.9 4.4 %collective-permute-start.5 = (f32[3,48,128]{2,1,0:T(8,128)S(1)}, f32[3,48,128]{2,1,0:T(8,128)S(1)}, u32[]{:S(2)}, u32[]{:S(2)}) collective-permute-start(f32[3,48,128]{2,1,0:T(8,128)S(1)} %get-tuple-element.18), channel_id=1, source_target_pairs={{0,3},{1,0},{2,1},{3,2},{4,7},{5,4},{6,5},{7,6},{8,11},{9,8},{10,9... | collective-permute-start | bytes 221192 | tf_op jit(solution)/shard_map/ppermute | solution.py:388

commit v3 on v2

--- a/solution.py
+++ b/solution.py
@@ -9,6 +9,7 @@
 AXES = ("gx", "gy", "gz")
 VM = pl.BlockSpec(memory_space=pltpu.VMEM)
 SM = pl.BlockSpec(memory_space=pltpu.SMEM)
+HB = pl.BlockSpec(memory_space=pltpu.HBM)
 F32 = jnp.float32
 
 NX, NY, NZ = 8, 32, 256
@@ -68,11 +69,27 @@
     return 0.5 / jnp.sqrt(top)
 
 
-def first_kernel(ratio, d, v, rho, energy, region, tracer, low, high, most, pressure):
+def first_kernel(
+    ratio, d, v, rho_in, energy_in, region_in, tracer_in,
+    low, high, most, pressure, rho, tracer, energy, region, sems,
+):
+    copies = []
+
+    def copy(src, dst):
+        cp = pltpu.make_async_copy(src, dst, sems.at[len(copies)])
+        cp.start()
+        copies.append(cp)
+
+    for pair in ((energy_in, energy), (region_in, region), (rho_in, rho), (tracer_in, tracer)):
+        copy(*pair)
     for f, array in enumerate((d, v)):
-        for table, size, out, shift in ((X_LOW, NL, low, NX), (X_HIGH, NH, high, -NX)):
-            for at, (c, x) in enumerate(table):
-                out[f * size + at] = array[c, x + shift]
+        for c in range(3):
+            n = 3 if c == 0 else 2
+            copy(array.at[c, pl.ds(NX - n, n)], low.at[pl.ds(f * NL + X_LOW.index((c, -n)), n)])
+            n = 4 if c == 0 else 2
+            copy(array.at[c, pl.ds(0, n)], high.at[pl.ds(f * NH + X_HIGH.index((c, NX)), n)])
+    for cp in copies[:4]:
+        cp.wait()
     top = jnp.zeros((MY, MZ), F32)
     for i in range(MX):
         reg = region[i]
@@ -92,6 +109,8 @@
     low[2 * NL + 1, :MY, :MZ] = tracer[MX - 1]
     top = jnp.max(jnp.max(top, axis=0, keepdims=True), axis=1, keepdims=True)
     most[...] = jnp.broadcast_to(top, most.shape)
+    for cp in copies[4:]:
+        cp.wait()
 
 
 def zone_plane(i, own, low, high, which):
@@ -285,34 +304,46 @@
                 new = v[c, x]
                 velocity[c, x] = new if force is None else new + gain[8 : 8 + NY, :NZ]
 
-    def sweep(ref, e):
-        now = ref[e]
-        total = ref[e - 1] + ref[e + 1]
-        total = total + (roll(now, 1, 0) + roll(now, -1, 0))
-        total = total + (roll(now, 1, 1) + roll(now, -1, 1))
-        return 0.1 * now + 0.15 * total
+    def sweep(ref, e, first, count, width):
+        rows = pl.ds(first, count)
+        now = ref[e, rows]
+        sides = roll(now, 1, 1) + roll(now, -1, 1)
+        rows_beside = ref[e, pl.ds(first - 1, count), :width] + ref[e, pl.ds(first + 1, count), :width]
+        planes_beside = ref[e - 1, rows, :width] + ref[e + 1, rows, :width]
+        total = planes_beside + rows_beside + sides[:, :width]
+        return 0.1 * now[:, :width] + 0.15 * total
 
     for e, (c, x) in enumerate(PLANES):
         if (c, x - 1) in PLANE_AT and (c, x + 1) in PLANE_AT:
-            once[e] = sweep(moved, e)
+            now = moved[e]
+            total = moved[e - 1] + moved[e + 1]
+            total = total + (roll(now, 1, 0) + roll(now, -1, 0))
+            total = total + (roll(now, 1, 1) + roll(now, -1, 1))
+            once[e] = 0.1 * now + 0.15 * total
     at = 0
     for e, (c, x) in enumerate(PLANES):
         inside = 0 <= x < NX
         if not inside and not (c == 0 and x in (-1, NX + 1)):
             continue
-        twice = sweep(once, e)
+        width = 384 if c == 2 and x % 2 else NZ
+        if c == 1 and x % 2:
+            edges = (sweep(once, e, 7, 1, width), sweep(once, e, 41, 1, width))
+        twice = sweep(once, e, 8, NY, width)
         if inside:
-            relaxed[c, x] = twice[8 : 8 + NY, :NZ]
+            relaxed[c, x] = twice[:, :NZ]
         if x % 2:
-            motion = twice - moved[e]
             first, count = (7, 18) if c == 1 else (9, 16)
-            for t in range(3):
+            for t in range(width // 128):
                 lanes = slice(128 * t, 128 * t + 128)
-                moves[t] = motion[:, lanes]
+                moves[t, pl.ds(8, NY), :] = twice[:, lanes] - moved[e, pl.ds(8, NY), lanes]
+                if c == 1:
+                    for row, edge in zip((7, 41), edges):
+                        moves[t, pl.ds(row, 1), :] = edge[:, lanes] - moved[e, pl.ds(row, 1), lanes]
                 gathered[pl.ds(at, count), lanes] = moves[t, pl.ds(first, count, stride=2), :]
             if c == 1:
                 gathered[pl.ds(at + 18, 6), :] = jnp.zeros((6, 384), F32)
             at += 24 if c == 1 else 16
+    gathered[pl.ds(0, (MX + 2) * 16 + MX * 24), NZ:] = jnp.zeros(((MX + 2) * 16 + MX * 24, 128), F32)
     n = lax.broadcasted_iota(jnp.int32, (384, 2 * MZ), 0)
     k = lax.broadcasted_iota(jnp.int32, (384, 2 * MZ), 1)
     node = jnp.where(n < 320, n, n - 384)
@@ -383,6 +414,10 @@
     return pltpu.with_memory_space_constraint(array, pltpu.VMEM)
 
 
+def in_hbm(array):
+    return pltpu.with_memory_space_constraint(array, pltpu.HBM)
+
+
 def moved_along(block, axis, by):
     n = lax.axis_size(axis)
     return on_chip(lax.ppermute(block, axis, [(i, (i + by) % n) for i in range(n)]))
@@ -401,22 +436,27 @@
 
 def on_device(displacement, velocity, density, energy, region, heat_ratio, tracer):
     n_devices = lax.axis_size(AXES)
-    displacement, velocity, density, energy, region, tracer = (
-        on_chip(array) for array in (displacement, velocity, density, energy, region, tracer)
-    )
-    low, high, most, pressure = pl.pallas_call(
+    low, high, most, pressure, density, tracer = pl.pallas_call(
         first_kernel,
         name="first",
         compiler_params=pltpu.CompilerParams(vmem_limit_bytes=8 << 20),
-        in_specs=[SM] + [VM] * 6,
-        out_specs=[VM] * 4,
+        in_specs=[SM] + [HB] * 6,
+        out_specs=[VM] * 6,
         out_shape=[
             local_of(2 * NL + 2, NY, NZ),
             local_of(2 * NH + 2, NY, NZ),
             local_of(n_devices, 128),
             local_of(MX, MY, MZ),
+            local_of(MX, MY, MZ),
+            local_of(MX, MY, MZ),
         ],
-    )(heat_ratio, displacement, velocity, density, energy, region, tracer)
+        scratch_shapes=[
+            pltpu.VMEM((MX, MY, MZ), F32),
+            pltpu.VMEM((MX, MY, MZ), jnp.int32),
+            pltpu.SemaphoreType.DMA((16,)),
+        ],
+    )(*map(in_hbm, (heat_ratio, displacement, velocity, density, energy, region, tracer)))
+    displacement, velocity = on_chip(displacement), on_chip(velocity)
     low = moved_along(low, "gx", 1)
     high = moved_along(high, "gx", -1)
     r = on_chip(lax.all_to_all(most, AXES, 0, 0, tiled=True))

time: 67.4 us -> 62.3 us (0.924)
  local copies, waits for them, and re-layouts: 6.62 us -> 0.67 us
  Pallas kernels: 8.33 us -> 9.53 us
    unnamed x24 -> x6, local copies, waits for them, and re-layouts: 6.62 us -> 0.67 us
    pallas_call x1, Pallas kernels: 1.36 us -> 2.86 us  [on_device(): pl.pallas_call(first_kernel, name='first', compiler_params=pltpu.Compiler...]
where the time goes in v3:
time: 62.3 us; the launch traced here: 62.2 us
  waiting for transfers between devices  29 us (47%)
  starting transfers between devices  22.3 us (36%)
  Pallas kernels  9.53 us (15%)
  between operations  0.71 us (1%)
  local copies, waits for them, and re-layouts  0.67 us (1%)
    ppermute x6, waiting for transfers between devices, moved_along(): lax.ppermute(block, axis, [(i, (i + by) % n) for i in range(n)])  29 us
    ppermute x6, starting transfers between devices, moved_along(): lax.ppermute(block, axis, [(i, (i + by) % n) for i in range(n)])  14.9 us
    all_to_all x1, starting transfers between devices, on_device(): r = on_chip(lax.all_to_all(most, AXES, 0, 0, tiled=True))  7.36 us
    pallas_call x1, Pallas kernels, on_device(): pl.pallas_call(last_kernel, name='last', compiler_params=pltpu.CompilerPa...  5.34 us
    pallas_call x1, Pallas kernels, on_device(): pl.pallas_call(first_kernel, name='first', compiler_params=pltpu.Compiler...  2.86 us
  transfers between devices with their start and end apart: 7, of which 4 were waited for; matrix products, arithmetic and copies ran while one was open for 0% of the time, Pallas kernels for 2%

profile of v3, /device:TPU:32, one launch (start us, length us, event | category | flops | bytes accessed | tf_op | source)
XLA Modules:
  0.0 62.2 jit_solution(15519108128007550853)
XLA Ops:
  0.6 0.0 copy-start.1
  0.6 0.0 copy-start
  0.7 2.9 %first.1 = (f32[16,32,256]{2,1,0:T(8,128)S(1)}, f32[18,32,256]{2,1,0:T(8,128)S(1)}, f32[256,128]{1,0:T(8,128)}, f32[4,16,128]{2,1,0:T(8,128)S(1)}, f32[4,16,128]{2,1,0:T(8,128)S(1)}, /*index=5*/f32[4,16,128]{2,1,0:T(8,128)S(1)}) custom-call(f32[4]{0:T(128)} %ratio.1, f32[3,8,32,256]{3,2,1,0:T(8,128)} %d.7, f32[3,8,32,256]{3,2,1,0:T(8,128)} %v.7, ...), custom_call_target="tpu_custom_call" | custom-call | tf_op jit(solution)/shard_map/first/pallas_call | solution.py:439
  3.5 0.1 collective-permute-start.1
  3.6 0.5 collective-permute-start
  4.1 13.7 %collective-permute-done.low = f32[16,32,256]{2,1,0:T(8,128)S(1)} collective-permute-done((f32[16,32,256]{2,1,0:T(8,128)S(1)}, f32[16,32,256]{2,1,0:T(8,128)S(1)}, u32[]{:S(2)}, u32[]{:S(2)}) %collective-permute-start) | collective-permute-done | bytes 524320 | tf_op jit(solution)/shard_map/ppermute | solution.py:423
  17.8 0.0 collective-permute-done.1.high
  17.8 0.0 copy-done.1
  17.8 0.0 copy-done
  17.8 0.1 second.1
  18.0 0.0 copy-start.2
  18.0 0.7 %copy-done.2 = f32[152,256]{1,0:T(8,128)} copy-done((f32[152,256]{1,0:T(8,128)}, f32[152,256]{1,0:T(8,128)S(1)}, u32[]{:S(2)}) %copy-start.2) | copy-done | bytes 155672
  18.6 8.0 %collective-permute-start.3 = (f32[184,256]{1,0:T(8,128)S(1)}, f32[184,256]{1,0:T(8,128)S(1)}, u32[]{:S(2)}, u32[]{:S(2)}) collective-permute-start(f32[184,256]{1,0:T(8,128)S(1)} %get-tuple-element.20), channel_id=1, source_target_pairs={{0,60},{4,0},{8,4},{12,8},{16,12},{20,16},{24,20},{28,24},{32,28},... | collective-permute-start | bytes 565256 | tf_op jit(solution)/shard_map/ppermute | solution.py:423
  26.7 7.4 %all-to-all-start = ((f32[256,1,128]{2,1,0:T(1,128)}), f32[256,1,128]{2,1,0:T(1,128)S(1)}, u32[]{:S(2)}, u32[]{:S(2)}) async-start(f32[256,1,128]{2,1,0:T(1,128)} %bitcast.1), calls=%async_computation | async-start | bytes 262144 | tf_op jit(solution)/shard_map/all_to_all | solution.py:462
  34.0 3.0 %collective-permute-start.2 = (f32[152,256]{1,0:T(8,128)}, f32[152,256]{1,0:T(8,128)S(1)}, u32[]{:S(2)}, u32[]{:S(2)}) collective-permute-start(f32[152,256]{1,0:T(8,128)} %copy-done.2), channel_id=1, source_target_pairs={{0,4},{4,8},{8,12},{12,16},{16,20},{20,24},{24,28},{28,32},{32,36}... | collective-permute-start | bytes 466952 | tf_op jit(solution)/shard_map/ppermute | solution.py:423
  37.0 12.7 %collective-permute-done.2.ylow = f32[152,256]{1,0:T(8,128)S(1)} collective-permute-done((f32[152,256]{1,0:T(8,128)}, f32[152,256]{1,0:T(8,128)S(1)}, u32[]{:S(2)}, u32[]{:S(2)}) %collective-permute-start.2) | collective-permute-done | bytes 155680 | tf_op jit(solution)/shard_map/ppermute | solution.py:423
  49.7 0.0 collective-permute-done.3.yhigh
  49.7 1.2 %third.1 = (f32[3,48,128]{2,1,0:T(8,128)S(1)}, f32[3,48,128]{2,1,0:T(8,128)S(1)}) custom-call(f32[3,8,32,256]{3,2,1,0:T(8,128)S(1)} %copy-done, f32[3,8,32,256]{3,2,1,0:T(8,128)S(1)} %copy-done.1, f32[16,32,256]{2,1,0:T(8,128)S(1)} %collective-permute-done.low, f32[18,32,256]{2,1,0:T(8,128)S(1)} %collective-permute-done.1.high, ...), custom_call_target="tpu_custom_call" | custom-call | tf_op jit(solution)/shard_map/third/pallas_call | solution.py:466
  50.9 1.6 %collective-permute-start.4 = (f32[3,48,128]{2,1,0:T(8,128)S(1)}, f32[3,48,128]{2,1,0:T(8,128)S(1)}, u32[]{:S(2)}, u32[]{:S(2)}) collective-permute-start(f32[3,48,128]{2,1,0:T(8,128)S(1)} %get-tuple-element.21), channel_id=1, source_target_pairs={{0,1},{1,2},{2,3},{3,0},{4,5},{5,6},{6,7},{7,4},{8,9},{9,10},{10,1... | collective-permute-start | bytes 221192 | tf_op jit(solution)/shard_map/ppermute | solution.py:423
  52.5 1.7 %collective-permute-start.5 = (f32[3,48,128]{2,1,0:T(8,128)S(1)}, f32[3,48,128]{2,1,0:T(8,128)S(1)}, u32[]{:S(2)}, u32[]{:S(2)}) collective-permute-start(f32[3,48,128]{2,1,0:T(8,128)S(1)} %get-tuple-element.22), channel_id=1, source_target_pairs={{0,3},{1,0},{2,1},{3,2},{4,7},{5,4},{6,5},{7,6},{8,11},{9,8},{10,9... | collective-permute-start | bytes 221192 | tf_op jit(solution)/shard_map/ppermute | solution.py:423
  54.2 0.0 all-to-all-done
  54.2 2.3 %collective-permute-done.4.zlow = f32[3,48,128]{2,1,0:T(8,128)S(1)} collective-permute-done((f32[3,48,128]{2,1,0:T(8,128)S(1)}, f32[3,48,128]{2,1,0:T(8,128)S(1)}, u32[]{:S(2)}, u32[]{:S(2)}) %collective-permute-start.4) | collective-permute-done | bytes 73760 | tf_op jit(solution)/shard_map/ppermute | solution.py:423
  56.5 0.3 collective-permute-done.5.zhigh
  56.8 5.3 %last.1 = (f32[3,8,32,256]{3,2,1,0:T(8,128)}, f32[3,8,32,256]{3,2,1,0:T(8,128)}, f32[4,16,128]{2,1,0:T(8,128)}) custom-call(f32[256,128]{1,0:T(8,128)S(1)} %bitcast.4, f32[3,8,32,256]{3,2,1,0:T(8,128)S(1)} %copy-done, f32[3,8,32,256]{3,2,1,0:T(8,128)S(1)} %copy-done.1, f32[16,32,256]{2,1,0:T(8,128)S(1)} %collective-permute-done.low, ...), custom_call_target="tpu_custom_call" | custom-call | tf_op jit(solution)/shard_map/last/pallas_call | solution.py:482
Async XLA Ops:
  0.6 17.2 %copy-start.1 = (f32[3,8,32,256]{3,2,1,0:T(8,128)S(1)}, f32[3,8,32,256]{3,2,1,0:T(8,128)}, u32[]{:S(2)}) copy-start(f32[3,8,32,256]{3,2,1,0:T(8,128)} %v.7) | copy-start | bytes 2359300
  0.6 17.2 %copy-start = (f32[3,8,32,256]{3,2,1,0:T(8,128)S(1)}, f32[3,8,32,256]{3,2,1,0:T(8,128)}, u32[]{:S(2)}) copy-start(f32[3,8,32,256]{3,2,1,0:T(8,128)} %d.7) | copy-start | bytes 2359300
  3.5 14.3 %collective-permute-start.1 = (f32[18,32,256]{2,1,0:T(8,128)S(1)}, f32[18,32,256]{2,1,0:T(8,128)S(1)}, u32[]{:S(2)}, u32[]{:S(2)}) collective-permute-start(f32[18,32,256]{2,1,0:T(8,128)S(1)} %get-tuple-element.15), channel_id=1, source_target_pairs={{0,192},{64,0},{128,64},{192,128},{1,193},{65,1},{129,65},{193,129... | collective-permute-start | bytes 1769480 | tf_op jit(solution)/shard_map/ppermute | solution.py:423
  3.6 14.2 %collective-permute-start = (f32[16,32,256]{2,1,0:T(8,128)S(1)}, f32[16,32,256]{2,1,0:T(8,128)S(1)}, u32[]{:S(2)}, u32[]{:S(2)}) collective-permute-start(f32[16,32,256]{2,1,0:T(8,128)S(1)} %get-tuple-element.14), channel_id=1, source_target_pairs={{0,64},{64,128},{128,192},{192,0},{1,65},{65,129},{129,193},{193,1... | collective-permute-start | bytes 1572872 | tf_op jit(solution)/shard_map/ppermute | solution.py:423
  18.0 0.7 %copy-start.2 = (f32[152,256]{1,0:T(8,128)}, f32[152,256]{1,0:T(8,128)S(1)}, u32[]{:S(2)}) copy-start(f32[152,256]{1,0:T(8,128)S(1)} %get-tuple-element.19) | copy-start | bytes 466948
  18.6 31.0 %collective-permute-start.3 = (f32[184,256]{1,0:T(8,128)S(1)}, f32[184,256]{1,0:T(8,128)S(1)}, u32[]{:S(2)}, u32[]{:S(2)}) collective-permute-start(f32[184,256]{1,0:T(8,128)S(1)} %get-tuple-element.20), channel_id=1, source_target_pairs={{0,60},{4,0},{8,4},{12,8},{16,12},{20,16},{24,20},{28,24},{32,28},... | collective-permute-start | bytes 565256 | tf_op jit(solution)/shard_map/ppermute | solution.py:423
  26.7 27.5 %all-to-all-start = ((f32[256,1,128]{2,1,0:T(1,128)}), f32[256,1,128]{2,1,0:T(1,128)S(1)}, u32[]{:S(2)}, u32[]{:S(2)}) async-start(f32[256,1,128]{2,1,0:T(1,128)} %bitcast.1), calls=%async_computation | async-start | bytes 262144 | tf_op jit(solution)/shard_map/all_to_all | solution.py:462
  34.0 15.6 %collective-permute-start.2 = (f32[152,256]{1,0:T(8,128)}, f32[152,256]{1,0:T(8,128)S(1)}, u32[]{:S(2)}, u32[]{:S(2)}) collective-permute-start(f32[152,256]{1,0:T(8,128)} %copy-done.2), channel_id=1, source_target_pairs={{0,4},{4,8},{8,12},{12,16},{16,20},{20,24},{24,28},{28,32},{32,36}... | collective-permute-start | bytes 466952 | tf_op jit(solution)/shard_map/ppermute | solution.py:423
  50.9 5.6 %collective-permute-start.4 = (f32[3,48,128]{2,1,0:T(8,128)S(1)}, f32[3,48,128]{2,1,0:T(8,128)S(1)}, u32[]{:S(2)}, u32[]{:S(2)}) collective-permute-start(f32[3,48,128]{2,1,0:T(8,128)S(1)} %get-tuple-element.21), channel_id=1, source_target_pairs={{0,1},{1,2},{2,3},{3,0},{4,5},{5,6},{6,7},{7,4},{8,9},{9,10},{10,1... | collective-permute-start | bytes 221192 | tf_op jit(solution)/shard_map/ppermute | solution.py:423
  52.5 4.4 %collective-permute-start.5 = (f32[3,48,128]{2,1,0:T(8,128)S(1)}, f32[3,48,128]{2,1,0:T(8,128)S(1)}, u32[]{:S(2)}, u32[]{:S(2)}) collective-permute-start(f32[3,48,128]{2,1,0:T(8,128)S(1)} %get-tuple-element.22), channel_id=1, source_target_pairs={{0,3},{1,0},{2,1},{3,2},{4,7},{5,4},{6,5},{7,6},{8,11},{9,8},{10,9... | collective-permute-start | bytes 221192 | tf_op jit(solution)/shard_map/ppermute | solution.py:423

commit v4 on v3

--- a/solution.py
+++ b/solution.py
@@ -6,7 +6,7 @@
 from jax.sharding import PartitionSpec as P
 
 
-AXES = ("gx", "gy", "gz")
+PEERS = ("gy", "gz")
 VM = pl.BlockSpec(memory_space=pltpu.VMEM)
 SM = pl.BlockSpec(memory_space=pltpu.SMEM)
 HB = pl.BlockSpec(memory_space=pltpu.HBM)
@@ -64,8 +64,11 @@
 Z_TILES = -(-(TRACER_SLOT + MX) // 32)
 
 
-def step_of(r):
-    top = jnp.max(jnp.max(r[...], axis=0, keepdims=True), axis=1, keepdims=True)
+def step_of(tops):
+    r = tops[0][...]
+    for other in tops[1:]:
+        r = jnp.maximum(r, other[...])
+    top = jnp.max(jnp.max(r, axis=0, keepdims=True), axis=1, keepdims=True)
     return 0.5 / jnp.sqrt(top)
 
 
@@ -219,11 +222,11 @@
 
 
 def last_kernel(
-    r, d, v, low, high, pressure, rho, tracer, ylow, yhigh, zlow, zhigh,
+    r0, r1, r2, r3, d, v, low, high, pressure, rho, tracer, ylow, yhigh, zlow, zhigh,
     velocity, relaxed, remapped,
     moved, once, pz, qx, qy, qz, qm, moves, gathered, result, tz,
 ):
-    step = step_of(r)
+    step = step_of((r0, r1, r2, r3))
     lane = lax.broadcasted_iota(jnp.int32, (1, 128), 1)
 
     def beside(slot, n, fill):
@@ -435,7 +438,7 @@
 
 
 def on_device(displacement, velocity, density, energy, region, heat_ratio, tracer):
-    n_devices = lax.axis_size(AXES)
+    n_peers = lax.axis_size(PEERS)
     low, high, most, pressure, density, tracer = pl.pallas_call(
         first_kernel,
         name="first",
@@ -445,7 +448,7 @@
         out_shape=[
             local_of(2 * NL + 2, NY, NZ),
             local_of(2 * NH + 2, NY, NZ),
-            local_of(n_devices, 128),
+            local_of(n_peers, 128),
             local_of(MX, MY, MZ),
             local_of(MX, MY, MZ),
             local_of(MX, MY, MZ),
@@ -459,7 +462,7 @@
     displacement, velocity = on_chip(displacement), on_chip(velocity)
     low = moved_along(low, "gx", 1)
     high = moved_along(high, "gx", -1)
-    r = on_chip(lax.all_to_all(most, AXES, 0, 0, tiled=True))
+    r = on_chip(lax.all_to_all(most, PEERS, 0, 0, tiled=True))
     ylow, yhigh = pack_y(displacement, velocity, low, high, pressure, density, tracer)
     ylow = moved_along(ylow, "gy", 1)
     yhigh = moved_along(yhigh, "gy", -1)
@@ -478,12 +481,15 @@
     )(displacement, velocity, low, high, pressure, density, tracer, ylow, yhigh)
     zlow = moved_along(zlow, "gz", 1)
     zhigh = moved_along(zhigh, "gz", -1)
+    tops = [r]
+    for by in (1, -1, 2):
+        tops.append(moved_along(r, "gx", by))
     q = pltpu.VMEM((3 * (MX + 4), 48, 128), F32)
     return pl.pallas_call(
         last_kernel,
         name="last",
         compiler_params=pltpu.CompilerParams(vmem_limit_bytes=30 << 20),
-        in_specs=[VM] * 12,
+        in_specs=[VM] * 15,
         out_specs=[VM] * 3,
         out_shape=[shape_of(3, NX, NY, NZ), shape_of(3, NX, NY, NZ), shape_of(MX, MY, MZ)],
         scratch_shapes=[
@@ -497,7 +503,7 @@
             pltpu.VMEM((MY + 16, MZ), F32),
         ],
     )(
-        r, displacement, velocity, low, high, pressure, density, tracer, ylow, yhigh, zlow, zhigh
+        *tops, displacement, velocity, low, high, pressure, density, tracer, ylow, yhigh, zlow, zhigh
     )
 
 

time: 62.3 us -> 61.2 us (0.982)
  the two profiles are of different devices: /device:TPU:32 before, /device:TPU:1 now
where the time goes in v4:
time: 61.2 us; the launch traced here: 61 us
  starting transfers between devices  29 us (47%)
  waiting for transfers between devices  21.8 us (36%)
  Pallas kernels  9.48 us (15%)
  between operations  0.69 us (1%)
    ppermute x9, starting transfers between devices, moved_along(): lax.ppermute(block, axis, [(i, (i + by) % n) for i in range(n)])  18.4 us
    ppermute x9, waiting for transfers between devices, moved_along(): lax.ppermute(block, axis, [(i, (i + by) % n) for i in range(n)])  15.8 us
    all_to_all x1, starting transfers between devices, on_device(): r = on_chip(lax.all_to_all(most, PEERS, 0, 0, tiled=True))  10.6 us
    all_to_all x1, waiting for transfers between devices, on_device(): r = on_chip(lax.all_to_all(most, PEERS, 0, 0, tiled=True))  6.01 us
    pallas_call x1, Pallas kernels, on_device(): pl.pallas_call(last_kernel, name='last', compiler_params=pltpu.CompilerPa...  5.33 us
    pallas_call x1, Pallas kernels, on_device(): pl.pallas_call(first_kernel, name='first', compiler_params=pltpu.Compiler...  2.82 us
  transfers between devices with their start and end apart: 10, of which 5 were waited for; matrix products, arithmetic and copies ran while one was open for 0% of the time, Pallas kernels for 2%

profile of v4, /device:TPU:1, one launch (start us, length us, event | category | flops | bytes accessed | tf_op | source)
XLA Modules:
  0.0 61.0 jit_solution(11153505546713045520)
XLA Ops:
  0.6 0.0 copy-start.1
  0.6 0.0 copy-start
  0.7 2.8 %first.1 = (f32[16,32,256]{2,1,0:T(8,128)S(1)}, f32[18,32,256]{2,1,0:T(8,128)S(1)}, f32[64,128]{1,0:T(8,128)}, f32[4,16,128]{2,1,0:T(8,128)S(1)}, f32[4,16,128]{2,1,0:T(8,128)S(1)}, /*index=5*/f32[4,16,128]{2,1,0:T(8,128)S(1)}) custom-call(f32[4]{0:T(128)} %ratio.1, f32[3,8,32,256]{3,2,1,0:T(8,128)} %d.7, f32[3,8,32,256]{3,2,1,0:T(8,128)} %v.7, ...), custom_call_target="tpu_custom_call" | custom-call | tf_op jit(solution)/shard_map/first/pallas_call | solution.py:442
  3.5 3.3 %collective-permute-start.4 = (f32[18,32,256]{2,1,0:T(8,128)S(1)}, f32[18,32,256]{2,1,0:T(8,128)S(1)}, u32[]{:S(2)}, u32[]{:S(2)}) collective-permute-start(f32[18,32,256]{2,1,0:T(8,128)S(1)} %get-tuple-element.15), channel_id=1, source_target_pairs={{0,192},{64,0},{128,64},{192,128},{1,193},{65,1},{129,65},{193,129... | collective-permute-start | bytes 1769480 | tf_op jit(solution)/shard_map/ppermute | solution.py:426
  6.8 0.0 collective-permute-start.3
  6.8 11.6 %collective-permute-done.3.low = f32[16,32,256]{2,1,0:T(8,128)S(1)} collective-permute-done((f32[16,32,256]{2,1,0:T(8,128)S(1)}, f32[16,32,256]{2,1,0:T(8,128)S(1)}, u32[]{:S(2)}, u32[]{:S(2)}) %collective-permute-start.3) | collective-permute-done | bytes 524320 | tf_op jit(solution)/shard_map/ppermute | solution.py:426
  18.3 1.1 %collective-permute-done.4.high = f32[18,32,256]{2,1,0:T(8,128)S(1)} collective-permute-done((f32[18,32,256]{2,1,0:T(8,128)S(1)}, f32[18,32,256]{2,1,0:T(8,128)S(1)}, u32[]{:S(2)}, u32[]{:S(2)}) %collective-permute-start.4) | collective-permute-done | bytes 589856 | tf_op jit(solution)/shard_map/ppermute | solution.py:426
  19.4 0.0 copy-done.1
  19.4 0.0 copy-done
  19.4 0.1 second.1
  19.6 8.2 %collective-permute-start.6 = (f32[184,256]{1,0:T(8,128)S(1)}, f32[184,256]{1,0:T(8,128)S(1)}, u32[]{:S(2)}, u32[]{:S(2)}) collective-permute-start(f32[184,256]{1,0:T(8,128)S(1)} %get-tuple-element.20), channel_id=1, source_target_pairs={{0,60},{4,0},{8,4},{12,8},{16,12},{20,16},{24,20},{28,24},{32,28},... | collective-permute-start | bytes 565256 | tf_op jit(solution)/shard_map/ppermute | solution.py:426
  27.8 0.0 collective-permute-start.5
  27.8 10.6 %all-to-all-start = ((f32[64,1,128]{2,1,0:T(1,128)}), f32[64,1,128]{2,1,0:T(1,128)S(1)}, u32[]{:S(2)}, u32[]{:S(2)}) async-start(f32[64,1,128]{2,1,0:T(1,128)} %bitcast.1), calls=%async_computation | async-start | bytes 65536 | tf_op jit(solution)/shard_map/all_to_all | solution.py:465
  38.4 0.6 %collective-permute-done.5.ylow = f32[152,256]{1,0:T(8,128)S(1)} collective-permute-done((f32[152,256]{1,0:T(8,128)S(1)}, f32[152,256]{1,0:T(8,128)S(1)}, u32[]{:S(2)}, u32[]{:S(2)}) %collective-permute-start.5) | collective-permute-done | bytes 155680 | tf_op jit(solution)/shard_map/ppermute | solution.py:426
  39.0 0.0 collective-permute-done.6.yhigh
  39.0 1.2 %third.1 = (f32[3,48,128]{2,1,0:T(8,128)S(1)}, f32[3,48,128]{2,1,0:T(8,128)S(1)}) custom-call(f32[3,8,32,256]{3,2,1,0:T(8,128)S(1)} %copy-done, f32[3,8,32,256]{3,2,1,0:T(8,128)S(1)} %copy-done.1, f32[16,32,256]{2,1,0:T(8,128)S(1)} %collective-permute-done.3.low, f32[18,32,256]{2,1,0:T(8,128)S(1)} %collective-permute-done.4.high, ...), custom_call_target="tpu_custom_call" | custom-call | tf_op jit(solution)/shard_map/third/pallas_call | solution.py:469
  40.2 1.4 %collective-permute-start.7 = (f32[3,48,128]{2,1,0:T(8,128)S(1)}, f32[3,48,128]{2,1,0:T(8,128)S(1)}, u32[]{:S(2)}, u32[]{:S(2)}) collective-permute-start(f32[3,48,128]{2,1,0:T(8,128)S(1)} %get-tuple-element.21), channel_id=1, source_target_pairs={{0,1},{1,2},{2,3},{3,0},{4,5},{5,6},{6,7},{7,4},{8,9},{9,10},{10,1... | collective-permute-start | bytes 221192 | tf_op jit(solution)/shard_map/ppermute | solution.py:426
  41.6 1.5 %collective-permute-start.8 = (f32[3,48,128]{2,1,0:T(8,128)S(1)}, f32[3,48,128]{2,1,0:T(8,128)S(1)}, u32[]{:S(2)}, u32[]{:S(2)}) collective-permute-start(f32[3,48,128]{2,1,0:T(8,128)S(1)} %get-tuple-element.22), channel_id=1, source_target_pairs={{0,3},{1,0},{2,1},{3,2},{4,7},{5,4},{6,5},{7,6},{8,11},{9,8},{10,9... | collective-permute-start | bytes 221192 | tf_op jit(solution)/shard_map/ppermute | solution.py:426
  43.1 6.0 %all-to-all-done = f32[64,1,128]{2,1,0:T(1,128)S(1)} async-done(((f32[64,1,128]{2,1,0:T(1,128)}), f32[64,1,128]{2,1,0:T(1,128)S(1)}, u32[]{:S(2)}, u32[]{:S(2)}) %all-to-all-start) | async-done | bytes 32800 | tf_op jit(solution)/shard_map/all_to_all | solution.py:465
  49.1 0.7 %collective-permute-start.2 = (f32[64,128]{1,0:T(8,128)S(1)}, f32[64,128]{1,0:T(8,128)S(1)}, u32[]{:S(2)}, u32[]{:S(2)}) collective-permute-start(f32[64,128]{1,0:T(8,128)S(1)} %bitcast.4), channel_id=1, source_target_pairs={{0,128},{64,192},{128,0},{192,64},{1,129},{65,193},{129,1},{193,65... | collective-permute-start | bytes 98312 | tf_op jit(solution)/shard_map/ppermute | solution.py:426
  49.9 2.7 %collective-permute-start.1 = (f32[64,128]{1,0:T(8,128)S(1)}, f32[64,128]{1,0:T(8,128)S(1)}, u32[]{:S(2)}, u32[]{:S(2)}) collective-permute-start(f32[64,128]{1,0:T(8,128)S(1)} %bitcast.5), channel_id=1, source_target_pairs={{0,192},{64,0},{128,64},{192,128},{1,193},{65,1},{129,65},{193,129... | collective-permute-start | bytes 98312 | tf_op jit(solution)/shard_map/ppermute | solution.py:426
  52.5 0.6 %collective-permute-start = (f32[64,128]{1,0:T(8,128)S(1)}, f32[64,128]{1,0:T(8,128)S(1)}, u32[]{:S(2)}, u32[]{:S(2)}) collective-permute-start(f32[64,128]{1,0:T(8,128)S(1)} %bitcast.6), channel_id=1, source_target_pairs={{0,64},{64,128},{128,192},{192,0},{1,65},{65,129},{129,193},{193,1... | collective-permute-start | bytes 98312 | tf_op jit(solution)/shard_map/ppermute | solution.py:426
  53.2 0.0 collective-permute-done.2.r3
  53.2 2.5 %collective-permute-done.1.r2 = f32[64,128]{1,0:T(8,128)S(1)} collective-permute-done((f32[64,128]{1,0:T(8,128)S(1)}, f32[64,128]{1,0:T(8,128)S(1)}, u32[]{:S(2)}, u32[]{:S(2)}) %collective-permute-start.1) | collective-permute-done | bytes 32800 | tf_op jit(solution)/shard_map/ppermute | solution.py:426
  55.7 0.0 collective-permute-done.r1
  55.7 0.0 collective-permute-done.7.zlow
  55.7 0.0 collective-permute-done.8.zhigh
  55.7 5.3 %last.1 = (f32[3,8,32,256]{3,2,1,0:T(8,128)}, f32[3,8,32,256]{3,2,1,0:T(8,128)}, f32[4,16,128]{2,1,0:T(8,128)}) custom-call(f32[64,128]{1,0:T(8,128)S(1)} %bitcast.7, f32[64,128]{1,0:T(8,128)S(1)} %collective-permute-done.r1, f32[64,128]{1,0:T(8,128)S(1)} %collective-permute-done.1.r2, f32[64,128]{1,0:T(8,128)S(1)} %collective-permute-done.2.r3, ...), custom_call_target="tpu_custom_call" | custom-call | tf_op jit(solution)/shard_map/last/pallas_call | solution.py:488
Async XLA Ops:
  0.6 18.8 %copy-start.1 = (f32[3,8,32,256]{3,2,1,0:T(8,128)S(1)}, f32[3,8,32,256]{3,2,1,0:T(8,128)}, u32[]{:S(2)}) copy-start(f32[3,8,32,256]{3,2,1,0:T(8,128)} %v.7) | copy-start | bytes 2359300
  0.6 18.8 %copy-start = (f32[3,8,32,256]{3,2,1,0:T(8,128)S(1)}, f32[3,8,32,256]{3,2,1,0:T(8,128)}, u32[]{:S(2)}) copy-start(f32[3,8,32,256]{3,2,1,0:T(8,128)} %d.7) | copy-start | bytes 2359300
  3.5 15.9 %collective-permute-start.4 = (f32[18,32,256]{2,1,0:T(8,128)S(1)}, f32[18,32,256]{2,1,0:T(8,128)S(1)}, u32[]{:S(2)}, u32[]{:S(2)}) collective-permute-start(f32[18,32,256]{2,1,0:T(8,128)S(1)} %get-tuple-element.15), channel_id=1, source_target_pairs={{0,192},{64,0},{128,64},{192,128},{1,193},{65,1},{129,65},{193,129... | collective-permute-start | bytes 1769480 | tf_op jit(solution)/shard_map/ppermute | solution.py:426
  6.8 11.6 %collective-permute-start.3 = (f32[16,32,256]{2,1,0:T(8,128)S(1)}, f32[16,32,256]{2,1,0:T(8,128)S(1)}, u32[]{:S(2)}, u32[]{:S(2)}) collective-permute-start(f32[16,32,256]{2,1,0:T(8,128)S(1)} %get-tuple-element.14), channel_id=1, source_target_pairs={{0,64},{64,128},{128,192},{192,0},{1,65},{65,129},{129,193},{193,1... | collective-permute-start | bytes 1572872 | tf_op jit(solution)/shard_map/ppermute | solution.py:426
  19.6 19.4 %collective-permute-start.6 = (f32[184,256]{1,0:T(8,128)S(1)}, f32[184,256]{1,0:T(8,128)S(1)}, u32[]{:S(2)}, u32[]{:S(2)}) collective-permute-start(f32[184,256]{1,0:T(8,128)S(1)} %get-tuple-element.20), channel_id=1, source_target_pairs={{0,60},{4,0},{8,4},{12,8},{16,12},{20,16},{24,20},{28,24},{32,28},... | collective-permute-start | bytes 565256 | tf_op jit(solution)/shard_map/ppermute | solution.py:426
  27.8 11.2 %collective-permute-start.5 = (f32[152,256]{1,0:T(8,128)S(1)}, f32[152,256]{1,0:T(8,128)S(1)}, u32[]{:S(2)}, u32[]{:S(2)}) collective-permute-start(f32[152,256]{1,0:T(8,128)S(1)} %get-tuple-element.19), channel_id=1, source_target_pairs={{0,4},{4,8},{8,12},{12,16},{16,20},{20,24},{24,28},{28,32},{32,36}... | collective-permute-start | bytes 466952 | tf_op jit(solution)/shard_map/ppermute | solution.py:426
  27.8 21.4 %all-to-all-start = ((f32[64,1,128]{2,1,0:T(1,128)}), f32[64,1,128]{2,1,0:T(1,128)S(1)}, u32[]{:S(2)}, u32[]{:S(2)}) async-start(f32[64,1,128]{2,1,0:T(1,128)} %bitcast.1), calls=%async_computation | async-start | bytes 65536 | tf_op jit(solution)/shard_map/all_to_all | solution.py:465
  40.2 15.4 %collective-permute-start.7 = (f32[3,48,128]{2,1,0:T(8,128)S(1)}, f32[3,48,128]{2,1,0:T(8,128)S(1)}, u32[]{:S(2)}, u32[]{:S(2)}) collective-permute-start(f32[3,48,128]{2,1,0:T(8,128)S(1)} %get-tuple-element.21), channel_id=1, source_target_pairs={{0,1},{1,2},{2,3},{3,0},{4,5},{5,6},{6,7},{7,4},{8,9},{9,10},{10,1... | collective-permute-start | bytes 221192 | tf_op jit(solution)/shard_map/ppermute | solution.py:426
  41.6 14.1 %collective-permute-start.8 = (f32[3,48,128]{2,1,0:T(8,128)S(1)}, f32[3,48,128]{2,1,0:T(8,128)S(1)}, u32[]{:S(2)}, u32[]{:S(2)}) collective-permute-start(f32[3,48,128]{2,1,0:T(8,128)S(1)} %get-tuple-element.22), channel_id=1, source_target_pairs={{0,3},{1,0},{2,1},{3,2},{4,7},{5,4},{6,5},{7,6},{8,11},{9,8},{10,9... | collective-permute-start | bytes 221192 | tf_op jit(solution)/shard_map/ppermute | solution.py:426
  49.1 4.0 %collective-permute-start.2 = (f32[64,128]{1,0:T(8,128)S(1)}, f32[64,128]{1,0:T(8,128)S(1)}, u32[]{:S(2)}, u32[]{:S(2)}) collective-permute-start(f32[64,128]{1,0:T(8,128)S(1)} %bitcast.4), channel_id=1, source_target_pairs={{0,128},{64,192},{128,0},{192,64},{1,129},{65,193},{129,1},{193,65... | collective-permute-start | bytes 98312 | tf_op jit(solution)/shard_map/ppermute | solution.py:426
  49.9 5.8 %collective-permute-start.1 = (f32[64,128]{1,0:T(8,128)S(1)}, f32[64,128]{1,0:T(8,128)S(1)}, u32[]{:S(2)}, u32[]{:S(2)}) collective-permute-start(f32[64,128]{1,0:T(8,128)S(1)} %bitcast.5), channel_id=1, source_target_pairs={{0,192},{64,0},{128,64},{192,128},{1,193},{65,1},{129,65},{193,129... | collective-permute-start | bytes 98312 | tf_op jit(solution)/shard_map/ppermute | solution.py:426
  52.5 3.1 %collective-permute-start = (f32[64,128]{1,0:T(8,128)S(1)}, f32[64,128]{1,0:T(8,128)S(1)}, u32[]{:S(2)}, u32[]{:S(2)}) collective-permute-start(f32[64,128]{1,0:T(8,128)S(1)} %bitcast.6), channel_id=1, source_target_pairs={{0,64},{64,128},{128,192},{192,0},{1,65},{65,129},{129,193},{193,1... | collective-permute-start | bytes 98312 | tf_op jit(solution)/shard_map/ppermute | solution.py:426
